TPU v7x, 512 devices: a whole 4x4x16 slice. The times are simulated.
512 devices in a mesh: seq: 64 (over y, z), head: 8 (over x, core).
Axes of the slice: x: 4, y: 4, z: 16, core: 2. Of those that a mesh axis runs over, the one named last changes fastest.
Arguments:
- queries: bfloat16 [32768, 4096], P(('seq', 'head')), may hold values from -8 to 8
- key_rows: bfloat16 [32768, 4096], P(('seq', 'head')), may hold values from -8 to 8
- value_rows: bfloat16 [32768, 4096], P(('seq', 'head')), may hold values from -8 to 8
- cotangent: bfloat16 [32768, 4096], P(('seq', 'head')), may hold values from -12 to 12
Outputs:
- attended: bfloat16 [32768, 4096], P(('seq', 'head'))
- grad_queries: bfloat16 [32768, 4096], P(('seq', 'head'))
- grad_keys: bfloat16 [32768, 4096], P(('seq', 'head'))
- grad_values: bfloat16 [32768, 4096], P(('seq', 'head'))
All inputs are finite; a program needn't handle non-finite values.
Results may differ from a plain program's by a relative error of at most 0.012.
Values may be sent and summed in bfloat16 or wider, within the bound.
No kernel may reach another device: no remote copies, remote signals or barrier semaphores. Data moves between devices by JAX's collectives and lax.ppermute only.
A program may use at most 128 MiB of HBM per device.

v0:
```python
import math

import jax
import jax.numpy as jnp
from jax import lax
from jax.sharding import PartitionSpec as P

HEAD_DIM = 128
BLOCK = 256


fill_low = -1e30
highest = lax.Precision.HIGHEST


def extended(array, sides, width):
    for axis, dim in sides:
        peers, length = (lax.axis_size(axis), array.shape[dim])
        up = [(i, (i + 1) % peers) for i in range(peers - 1)]
        down = [(j, i) for i, j in up]
        last = lax.slice_in_dim(array, length - width, length, axis=dim)
        first = lax.slice_in_dim(array, 0, width, axis=dim)
        before = lax.ppermute(last, axis, up)
        after = lax.ppermute(first, axis, down)
        array = jnp.concatenate([before, array, after], axis=dim)
    return array


def partner(array, axis, distance):
    return lax.ppermute(array, axis, [(i, i ^ 1 << distance) for i in range(lax.axis_size(axis))])


def coarsen(matrix):
    paired = matrix.reshape(matrix.shape[0] // 2, 2, matrix.shape[1]).astype(jnp.float32)
    return ((paired[:, 0] + paired[:, 1]) * 0.5).astype(jnp.bfloat16)


def to_heads(statistic):
    return jnp.transpose(statistic, (1, 0, 2)).reshape(statistic.shape[1], -1)


def to_groups(statistic, groups):
    return jnp.transpose(statistic.reshape(statistic.shape[0], groups, -1), (1, 0, 2))


def add_edges(matrix, lower_term, upper_term, block_rows):
    return jnp.concatenate(
        [
            matrix[:block_rows] + lower_term,
            matrix[block_rows:-block_rows],
            matrix[-block_rows:] + upper_term,
        ],
        axis=0,
    )


def descend(grads):
    running = grads[-1]
    for height in range(len(grads) - 1, 0, -1):
        running = grads[height - 1] + jnp.repeat(running * 0.5, 2, axis=0)
    return running


def per_device(queries, key_rows, value_rows, cotangent):
    own_query, own_keys, own_values, upstream = (
        lax.all_to_all(queries, "head", split_axis=1, concat_axis=0, tiled=True),
        lax.all_to_all(key_rows, "head", split_axis=1, concat_axis=0, tiled=True),
        lax.all_to_all(value_rows, "head", split_axis=1, concat_axis=0, tiled=True),
        lax.all_to_all(cotangent, "head", split_axis=1, concat_axis=0, tiled=True),
    )
    row_count, features = own_query.shape
    head_dim = HEAD_DIM
    head_count = features // head_dim
    block_rows = BLOCK
    block_count = row_count // block_rows
    shard_count = lax.axis_size("seq")
    seq_bits = shard_count.bit_length() - 1
    base_level = block_count.bit_length() - 1
    top_level = base_level + seq_bits - 1
    seq_pos = lax.axis_index("seq")
    score_scale = 1.0 / math.sqrt(head_dim)
    key_value = jnp.concatenate([own_keys, own_values], axis=1)
    query_levels = [own_query]
    pair_levels = [key_value]
    for height in range(1, top_level + 1):
        query_levels.append(coarsen(query_levels[-1]))
        pair_levels.append(coarsen(pair_levels[-1]))
    pair_ext = extended(key_value, (("seq", 0),), block_rows)
    stacked = pair_ext.reshape(block_count + 2, block_rows, 2 * features)
    window = jnp.concatenate([stacked[:-2], stacked[1:-1], stacked[2:]], axis=1)
    key_win = window[:, :, :features].reshape(block_count, 3 * block_rows, head_count, head_dim)
    value_win = window[:, :, features:].reshape(block_count, 3 * block_rows, head_count, head_dim)
    global_block = seq_pos * block_count + jnp.arange(block_count)
    columns = jnp.arange(3 * block_rows)
    valid_mask = (
        ((columns[None, :] >= block_rows) | (global_block[:, None] > 0))
        & (
            (columns[None, :] < 2 * block_rows)
            | (global_block[:, None] < block_count * shard_count - 1)
        )
    )[:, None, None, :]
    query_blk = own_query.reshape(block_count, block_rows, head_count, head_dim)
    grad_blk = upstream.reshape(block_count, block_rows, head_count, head_dim)
    near_scores = (
        jnp.einsum("bihd,bjhd->bhij", query_blk, key_win, preferred_element_type=jnp.float32)
        * score_scale
    )
    row_max = to_heads(jnp.max(jnp.where(valid_mask, near_scores, fill_low), axis=3))
    level_list = []
    group_pairs = pair_levels[base_level]
    for bit_pos in range(seq_bits):
        sibling = partner(group_pairs, "seq", bit_pos)
        level_list.append((base_level + bit_pos, sibling[None]))
        if bit_pos + 1 < seq_bits:
            lower_half = seq_pos // 2**bit_pos % 2 == 0
            joined = jnp.where(
                lower_half,
                jnp.concatenate([group_pairs, sibling], axis=0),
                jnp.concatenate([sibling, group_pairs], axis=0),
            )
            group_pairs = coarsen(joined)
    level_scores = []
    for height, pair_blk in level_list:
        groups = pair_blk.shape[0]
        coarse_query = query_levels[height].reshape(groups, -1, head_count, head_dim)
        key_blk = pair_blk[:, :, :features].reshape(groups, block_rows, head_count, head_dim)
        coarse_scores = (
            jnp.einsum("grhd,gjhd->ghrj", coarse_query, key_blk, preferred_element_type=jnp.float32)
            * score_scale
        )
        level_scores.append(coarse_scores)
        row_max = jnp.maximum(
            row_max, jnp.repeat(to_heads(jnp.max(coarse_scores, axis=3)), 2**height, axis=1)
        )
    near_weights = jnp.where(
        valid_mask, jnp.exp(near_scores - to_groups(row_max, block_count)[..., None]), 0.0
    )
    totals = to_heads(jnp.sum(near_weights, axis=3))
    numerator = jnp.einsum(
        "bhij,bjhd->bihd",
        near_weights.astype(jnp.bfloat16),
        value_win,
        preferred_element_type=jnp.float32,
    ).reshape(row_count, head_count, head_dim)
    level_terms = []
    for (height, pair_blk), coarse_scores in zip(level_list, level_scores):
        groups = pair_blk.shape[0]
        repeat = 2**height
        value_blk = pair_blk[:, :, features:].reshape(groups, block_rows, head_count, head_dim)
        coarse_max = jnp.min(row_max.reshape(head_count, -1, repeat), axis=2)
        coarse_weights = 2.0**height * jnp.exp(
            coarse_scores - to_groups(coarse_max, groups)[..., None]
        )
        rescale = jnp.exp(jnp.repeat(coarse_max, repeat, axis=1) - row_max)
        totals = totals + rescale * jnp.repeat(
            to_heads(jnp.sum(coarse_weights, axis=3)), repeat, axis=1
        )
        rounded_coarse = coarse_weights.astype(jnp.bfloat16)
        coarse_part = jnp.einsum(
            "ghrj,gjhd->grhd", rounded_coarse, value_blk, preferred_element_type=jnp.float32
        ).reshape(row_count // repeat, head_count, head_dim)
        numerator = (
            numerator + jnp.repeat(coarse_part, repeat, axis=0) * jnp.transpose(rescale)[:, :, None]
        )
        level_terms.append((coarse_weights, rounded_coarse, rescale))
    attended_f = numerator / jnp.transpose(totals)[:, :, None]
    attended = attended_f.reshape(row_count, features).astype(jnp.bfloat16)
    grad_heads = upstream.reshape(row_count, head_count, head_dim).astype(jnp.float32)
    delta_rows = jnp.sum(grad_heads * attended_f, axis=2)
    delta_heads = jnp.transpose(delta_rows)
    near_share = near_weights / to_groups(totals, block_count)[..., None]
    near_prod = jnp.einsum(
        "bihd,bjhd->bhij", grad_blk, value_win, preferred_element_type=jnp.float32
    )
    near_grad = (
        near_share * (near_prod - to_groups(delta_heads, block_count)[..., None]) * score_scale
    ).astype(jnp.bfloat16)
    query_grad0 = jnp.einsum(
        "bhij,bjhd->bihd", near_grad, key_win, preferred_element_type=jnp.float32
    ).reshape(row_count, features)
    key_grad_win = jnp.einsum(
        "bhij,bihd->bjhd", near_grad, query_blk, preferred_element_type=jnp.float32
    ).reshape(block_count, 3 * block_rows, features)
    value_grad_win = jnp.einsum(
        "bhij,bihd->bjhd",
        near_share.astype(jnp.bfloat16),
        grad_blk,
        preferred_element_type=jnp.float32,
    ).reshape(block_count, 3 * block_rows, features)
    pair_grad_win = jnp.concatenate([key_grad_win, value_grad_win], axis=2)
    ext_grad = jnp.pad(pair_grad_win[:, :block_rows], ((0, 2), (0, 0), (0, 0)))
    ext_grad = ext_grad + jnp.pad(
        pair_grad_win[:, block_rows : 2 * block_rows], ((1, 1), (0, 0), (0, 0))
    )
    ext_grad = ext_grad + jnp.pad(pair_grad_win[:, 2 * block_rows :], ((2, 0), (0, 0), (0, 0)))
    pair_grad0 = ext_grad[1:-1].reshape(row_count, 2 * features)
    rim_rows = jnp.concatenate([ext_grad[0], ext_grad[-1]], axis=0)
    returned = extended(rim_rows, (("seq", 0),), block_rows)
    lower_term = returned[:block_rows]
    upper_term = returned[-block_rows:]
    pair_grad0 = add_edges(pair_grad0, lower_term, upper_term, block_rows)
    query_grads = [query_grad0] + [
        jnp.zeros((row_count // 2**height, features), jnp.float32)
        for height in range(1, top_level + 1)
    ]
    pair_grads = [pair_grad0] + [
        jnp.zeros((row_count // 2**height, 2 * features), jnp.float32)
        for height in range(1, top_level + 1)
    ]
    cross_grads = []
    for (height, pair_blk), (coarse_weights, rounded_coarse, rescale) in zip(
        level_list, level_terms
    ):
        groups = pair_blk.shape[0]
        repeat = 2**height
        scaled = rescale / totals
        pooled = jnp.sum(
            (grad_heads * jnp.transpose(scaled)[:, :, None]).reshape(
                row_count // repeat, repeat, head_count, head_dim
            ),
            axis=1,
        )
        pooled_delta = jnp.sum((delta_heads * scaled).reshape(head_count, -1, repeat), axis=2)
        pooled_blk = pooled.reshape(groups, -1, head_count, head_dim)
        key_blk = pair_blk[:, :, :features].reshape(groups, block_rows, head_count, head_dim)
        value_f = (
            pair_blk[:, :, features:]
            .reshape(groups, block_rows, head_count, head_dim)
            .astype(jnp.float32)
        )
        grad_prod = jnp.einsum("grhd,gjhd->ghrj", pooled_blk, value_f, precision=highest)
        coarse_grad = (
            coarse_weights * (grad_prod - to_groups(pooled_delta, groups)[..., None]) * score_scale
        ).astype(jnp.bfloat16)
        coarse_query_grad = jnp.einsum(
            "ghrj,gjhd->grhd", coarse_grad, key_blk, preferred_element_type=jnp.float32
        ).reshape(row_count // repeat, features)
        query_grads[height] = coarse_query_grad
        coarse_query = query_levels[height].reshape(groups, -1, head_count, head_dim)
        key_part = jnp.einsum(
            "ghrj,grhd->gjhd", coarse_grad, coarse_query, preferred_element_type=jnp.float32
        ).reshape(groups, block_rows, features)
        value_part = jnp.einsum(
            "ghrj,grhd->gjhd", rounded_coarse.astype(jnp.float32), pooled_blk, precision=highest
        ).reshape(groups, block_rows, features)
        pair_part = jnp.concatenate([key_part, value_part], axis=2)
        cross_grads.append(pair_part[0])
    group_grad = jnp.zeros((block_rows, 2 * features), jnp.float32)
    for bit_pos in reversed(range(seq_bits)):
        if bit_pos + 1 < seq_bits:
            lower_half = seq_pos // 2**bit_pos % 2 == 0
            doubled = jnp.repeat(group_grad * 0.5, 2, axis=0)
            own_part = jnp.where(lower_half, doubled[:block_rows], doubled[block_rows:])
            far_part = jnp.where(lower_half, doubled[block_rows:], doubled[:block_rows])
        else:
            own_part = jnp.zeros((block_rows, 2 * features), jnp.float32)
            far_part = jnp.zeros((block_rows, 2 * features), jnp.float32)
        returned_grad = partner(cross_grads[bit_pos] + far_part, "seq", bit_pos)
        group_grad = own_part + returned_grad
    pair_grads[base_level] = group_grad
    grad_query = descend(query_grads).astype(jnp.bfloat16)
    pair_total = descend(pair_grads)
    grad_key = pair_total[:, :features].astype(jnp.bfloat16)
    grad_value = pair_total[:, features:].astype(jnp.bfloat16)
    return (
        lax.all_to_all(attended, "head", split_axis=0, concat_axis=1, tiled=True),
        lax.all_to_all(grad_query, "head", split_axis=0, concat_axis=1, tiled=True),
        lax.all_to_all(grad_key, "head", split_axis=0, concat_axis=1, tiled=True),
        lax.all_to_all(grad_value, "head", split_axis=0, concat_axis=1, tiled=True),
    )


def solution(mesh):
    return jax.shard_map(
        per_device,
        mesh=mesh,
        in_specs=(
            P(("seq", "head"), None),
            P(("seq", "head"), None),
            P(("seq", "head"), None),
            P(("seq", "head"), None),
        ),
        out_specs=(
            P(("seq", "head"), None),
            P(("seq", "head"), None),
            P(("seq", "head"), None),
            P(("seq", "head"), None),
        ),
        check_vma=False,
    )
```

profile of v0, /device:TPU:1, one launch (start us, length us, event | category | flops | bytes accessed | tf_op | source)
XLA Modules:
  0.0 963.2 jit_solution(3167091999867492557)
XLA Ops:
  2.6 10.4 %all-to-all-start = ((bf16[64,8,512]{2,0,1:T(8,128)(2,1)}), bf16[64,8,512]{2,0,1:T(8,128)(2,1)S(1)}, u32[]{:S(2)}, u32[]{:S(2)}) async-start(bf16[64,8,512]{2,0,1:T(8,128)(2,1)} %bitcast.530), calls=%async_computation | async-start | bytes 1048576 | tf_op jit(solution)/shard_map/all_to_all | solution.py:67
  13.8 8.5 all-to-all-done
  22.4 4.4 all-to-all-start.1
  28.7 7.4 all-to-all-done.1
  36.1 4.4 all-to-all-start.2
  46.0 3.8 all-to-all-done.2
  49.9 4.4 all-to-all-start.4
  84.2 3.3 fusion.41
  87.5 3.4 reshape.1277
  90.9 3.8 fusion.58
  95.7 2.5 collective-permute-start.3
  101.9 2.6 copy.996
  104.5 18.0 %collective-permute-done.3 = bf16[256,1024]{1,0:T(8,128)(2,1)} collective-permute-done((bf16[256,1024]{1,0:T(8,128)(2,1)}, bf16[256,1024]{1,0:T(8,128)(2,1)}, u32[]{:S(2)}, u32[]{:S(2)}) %collective-permute-start.3) | collective-permute-done | bytes 524320 | tf_op jit(solution)/shard_map/ppermute | solution.py:30
  122.5 3.4 fusion.42
  125.9 3.4 reshape.1279
  129.3 3.8 fusion.59
  134.0 6.9 collective-permute-start.4
  141.0 3.5 select_reduce_fusion
  151.7 2.6 copy.995
  155.9 30.8 %collective-permute-done.4 = bf16[256,1024]{1,0:T(8,128)(2,1)} collective-permute-done((bf16[256,1024]{1,0:T(8,128)(2,1)}, bf16[256,1024]{1,0:T(8,128)(2,1)}, u32[]{:S(2)}, u32[]{:S(2)}) %collective-permute-start.4) | collective-permute-done | bytes 524320 | tf_op jit(solution)/shard_map/ppermute | solution.py:30
  186.7 3.4 fusion.43
  190.0 3.4 reshape.1281
  193.5 3.7 fusion.60
  198.1 13.7 %collective-permute-start.5 = (bf16[256,1024]{1,0:T(8,128)(2,1)}, bf16[256,1024]{1,0:T(8,128)(2,1)}, u32[]{:S(2)}, u32[]{:S(2)}) collective-permute-start(bf16[256,1024]{1,0:T(8,128)(2,1)} %bitcast.533), channel_id=1, source_target_pairs={{0,64},{8,72},{16,80},{24,88},{32,96},{40,104},{48,112},{56,120},{... | collective-permute-start | bytes 1572872 | tf_op jit(solution)/shard_map/ppermute | solution.py:30
  224.6 26.8 %collective-permute-done.5 = bf16[256,1024]{1,0:T(8,128)(2,1)} collective-permute-done((bf16[256,1024]{1,0:T(8,128)(2,1)}, bf16[256,1024]{1,0:T(8,128)(2,1)}, u32[]{:S(2)}, u32[]{:S(2)}) %collective-permute-start.5) | collective-permute-done | bytes 524320 | tf_op jit(solution)/shard_map/ppermute | solution.py:30
  251.4 3.3 fusion.44
  254.8 3.4 reshape.1283
  258.2 3.7 fusion.61
  262.9 3.1 collective-permute-start.6
  278.1 3.4 fusion.45
  281.5 3.4 reshape.1285
  284.9 3.7 fusion.62
  289.6 4.7 collective-permute-start.7
  345.4 3.1 maximum_reduce_fusion.1
  433.8 3.6 bitcast_reduce_fusion
  438.1 6.4 fusion.4
  444.5 3.6 copy.1160
  452.3 5.6 fusion.13
  457.9 2.5 copy.1111
  490.4 7.2 fusion.51
  504.1 6.0 fusion.1
  510.1 2.9 fusion.204
  513.0 3.5 copy.1159
  516.5 2.7 fusion.11
  531.1 2.6 multiply_reduce_fusion.4
  564.6 2.6 mul.561
  581.1 6.4 collective-permute-start.10
  600.0 8.8 collective-permute-done.10
  616.7 4.9 collective-permute-start.11
  635.6 6.8 collective-permute-done.11
  650.4 5.4 collective-permute-start.12
  669.8 52.1 %collective-permute-done.12 = f32[256,1024]{1,0:T(8,128)} collective-permute-done((f32[256,1024]{1,0:T(8,128)}, f32[256,1024]{1,0:T(8,128)}, u32[]{:S(2)}, u32[]{:S(2)}) %collective-permute-start.12) | collective-permute-done | bytes 1048608 | tf_op jit(solution)/shard_map/ppermute | solution.py:30
  732.8 83.6 %collective-permute-done.13 = f32[256,1024]{1,0:T(8,128)} collective-permute-done((f32[256,1024]{1,0:T(8,128)}, f32[256,1024]{1,0:T(8,128)}, u32[]{:S(2)}, u32[]{:S(2)}) %collective-permute-start.13) | collective-permute-done | bytes 1048608 | tf_op jit(solution)/shard_map/ppermute | solution.py:30
  828.8 3.5 convolution_bitcast_fusion
  836.5 31.6 %collective-permute-done.14 = f32[256,1024]{1,0:T(8,128)} collective-permute-done((f32[256,1024]{1,0:T(8,128)}, f32[256,1024]{1,0:T(8,128)}, u32[]{:S(2)}, u32[]{:S(2)}) %collective-permute-start.14) | collective-permute-done | bytes 1048608 | tf_op jit(solution)/shard_map/ppermute | solution.py:30
  877.6 4.9 all-to-all-start.5
  903.8 6.6 divide_convert_fusion
  910.4 3.0 fusion.34
  918.3 2.7 reshape.1274
  921.0 4.8 all-to-all-start.3
  928.3 7.1 all-to-all-done.3
  935.3 12.7 %all_to_all.140 = bf16[8,64,512]{2,1,0:T(8,128)(2,1)S(1)} all-to-all(bf16[8,64,512]{2,1,0:T(8,128)(2,1)S(1)} %bitcast.603), channel_id=1, replica_groups=mesh['seq'=64,'head'=8] {'head'}, dimensions={0} | all-to-all | bytes 1048576 | tf_op jit(solution)/shard_map/all_to_all | solution.py:268
  948.0 4.4 all-to-all-start.7
  957.0 4.8 all-to-all-done.7
  (650 shorter events, 442.4 us)
Async XLA Ops:
  0.6 12.4 %copy-start.69 = (bf16[64,4096]{1,0:T(8,128)(2,1)S(1)}, bf16[64,4096]{1,0:T(8,128)(2,1)}, u32[]{:S(2)}) copy-start(bf16[64,4096]{1,0:T(8,128)(2,1)} %param.6) | copy-start | bytes 1572868
  0.6 26.1 %copy-start.70 = (bf16[64,4096]{1,0:T(8,128)(2,1)S(1)}, bf16[64,4096]{1,0:T(8,128)(2,1)}, u32[]{:S(2)}) copy-start(bf16[64,4096]{1,0:T(8,128)(2,1)} %param.4) | copy-start | bytes 1572868
  2.6 25.0 %copy-start.71 = (bf16[64,4096]{1,0:T(8,128)(2,1)S(1)}, bf16[64,4096]{1,0:T(8,128)(2,1)}, u32[]{:S(2)}) copy-start(bf16[64,4096]{1,0:T(8,128)(2,1)} %param.7) | copy-start | bytes 1572868
  2.6 19.7 %all-to-all-start = ((bf16[64,8,512]{2,0,1:T(8,128)(2,1)}), bf16[64,8,512]{2,0,1:T(8,128)(2,1)S(1)}, u32[]{:S(2)}, u32[]{:S(2)}) async-start(bf16[64,8,512]{2,0,1:T(8,128)(2,1)} %bitcast.530), calls=%async_computation | async-start | bytes 1048576 | tf_op jit(solution)/shard_map/all_to_all | solution.py:67
  22.4 13.7 %all-to-all-start.1 = ((bf16[64,8,512]{2,0,1:T(8,128)(2,1)}), bf16[64,8,512]{2,0,1:T(8,128)(2,1)S(1)}, u32[]{:S(2)}, u32[]{:S(2)}) async-start(bf16[64,8,512]{2,0,1:T(8,128)(2,1)} %bitcast.529), calls=%async_computation.1 | async-start | bytes 1048576 | tf_op jit(solution)/shard_map/all_to_all | solution.py:68
  28.5 112.5 %copy-start.103 = (pred[2,768]{1,0:T(4,128)(4,1)}, pred[2,768]{1,0:T(4,128)(4,1)S(1)}, u32[]{:S(2)}) copy-start(pred[2,768]{1,0:T(4,128)(4,1)S(1)} %or_and_fusion) | copy-start | bytes 4612
  36.1 13.7 %all-to-all-start.2 = ((bf16[64,8,512]{2,0,1:T(8,128)(2,1)}), bf16[64,8,512]{2,0,1:T(8,128)(2,1)S(1)}, u32[]{:S(2)}, u32[]{:S(2)}) async-start(bf16[64,8,512]{2,0,1:T(8,128)(2,1)} %bitcast.528), calls=%async_computation.2 | async-start | bytes 1048576 | tf_op jit(solution)/shard_map/all_to_all | solution.py:66
  44.1 40.1 %collective-permute-start.2 = (bf16[256,1024]{1,0:T(8,128)(2,1)}, bf16[256,1024]{1,0:T(8,128)(2,1)}, u32[]{:S(2)}, u32[]{:S(2)}) collective-permute-start(bf16[256,1024]{1,0:T(8,128)(2,1)} %bitcast.536), channel_id=1, source_target_pairs={{0,8},{8,0},{16,24},{24,16},{32,40},{40,32},{48,56},{56,48},{64,72... | collective-permute-start | bytes 1572872 | tf_op jit(solution)/shard_map/ppermute | solution.py:30
  49.9 13.7 %all-to-all-start.4 = ((bf16[64,8,512]{2,0,1:T(8,128)(2,1)}), bf16[64,8,512]{2,0,1:T(8,128)(2,1)S(1)}, u32[]{:S(2)}, u32[]{:S(2)}) async-start(bf16[64,8,512]{2,0,1:T(8,128)(2,1)} %bitcast.591), calls=%async_computation.4 | async-start | bytes 1048576 | tf_op jit(solution)/shard_map/all_to_all | solution.py:69
  66.0 147.7 %copy-start.50 = (bf16[128,1,512]{0,2,1:T(8,128)(2,1)}, bf16[128,1,512]{0,2,1:T(8,128)(2,1)S(1)}, u32[]{:S(2)}) copy-start(bf16[128,1,512]{0,2,1:T(8,128)(2,1)S(1)} %copy.1010) | copy-start | bytes 393220
  74.7 23.5 %collective-permute-start = (bf16[256,1024]{1,0:T(8,128)(2,1)}, bf16[256,1024]{1,0:T(8,128)(2,1)}, u32[]{:S(2)}, u32[]{:S(2)}) collective-permute-start(bf16[256,1024]{1,0:T(8,128)(2,1)} %get-tuple-element.50), channel_id=1, source_target_pairs={{0,8},{8,16},{16,24},{24,32},{32,40},{40,48},{48,56},{56,64},{64,7... | collective-permute-start | bytes 1572872 | tf_op jit(solution)/shard_map/ppermute | solution.py:23
  76.8 21.4 %collective-permute-start.1 = (bf16[256,1024]{1,0:T(8,128)(2,1)}, bf16[256,1024]{1,0:T(8,128)(2,1)}, u32[]{:S(2)}, u32[]{:S(2)}) collective-permute-start(bf16[256,1024]{1,0:T(8,128)(2,1)} %get-tuple-element.51), channel_id=1, source_target_pairs={{8,0},{16,8},{24,16},{32,24},{40,32},{48,40},{56,48},{64,56},{72,6... | collective-permute-start | bytes 1572872 | tf_op jit(solution)/shard_map/ppermute | solution.py:24
  80.5 60.5 %copy-start.7 = (bf16[2,256,4,128]{1,3,2,0:T(8,128)(2,1)}, bf16[2,256,4,128]{1,3,2,0:T(8,128)(2,1)S(1)}, u32[]{:S(2)}) copy-start(bf16[2,256,4,128]{1,3,2,0:T(8,128)(2,1)S(1)} %copy.1156) | copy-start | bytes 1572868
  95.7 26.9 %collective-permute-start.3 = (bf16[256,1024]{1,0:T(8,128)(2,1)}, bf16[256,1024]{1,0:T(8,128)(2,1)}, u32[]{:S(2)}, u32[]{:S(2)}) collective-permute-start(bf16[256,1024]{1,0:T(8,128)(2,1)} %bitcast.535), channel_id=1, source_target_pairs={{0,16},{8,24},{16,0},{24,8},{32,48},{40,56},{48,32},{56,40},{64,80... | collective-permute-start | bytes 1572872 | tf_op jit(solution)/shard_map/ppermute | solution.py:30
  129.3 11.7 %copy-start.4 = (bf16[2,768,512]{1,2,0:T(8,128)(2,1)S(1)}, bf16[2,768,512]{1,2,0:T(8,128)(2,1)}, u32[]{:S(2)}) copy-start(bf16[2,768,512]{1,2,0:T(8,128)(2,1)} %copy.996) | copy-start | bytes 4718596
  134.0 52.6 %collective-permute-start.4 = (bf16[256,1024]{1,0:T(8,128)(2,1)}, bf16[256,1024]{1,0:T(8,128)(2,1)}, u32[]{:S(2)}, u32[]{:S(2)}) collective-permute-start(bf16[256,1024]{1,0:T(8,128)(2,1)} %bitcast.534), channel_id=1, source_target_pairs={{0,32},{8,40},{16,48},{24,56},{32,0},{40,8},{48,16},{56,24},{64,96... | collective-permute-start | bytes 1572872 | tf_op jit(solution)/shard_map/ppermute | solution.py:30
  141.0 6.3 copy-start.35
  198.1 53.3 %collective-permute-start.5 = (bf16[256,1024]{1,0:T(8,128)(2,1)}, bf16[256,1024]{1,0:T(8,128)(2,1)}, u32[]{:S(2)}, u32[]{:S(2)}) collective-permute-start(bf16[256,1024]{1,0:T(8,128)(2,1)} %bitcast.533), channel_id=1, source_target_pairs={{0,64},{8,72},{16,80},{24,88},{32,96},{40,104},{48,112},{56,120},{... | collective-permute-start | bytes 1572872 | tf_op jit(solution)/shard_map/ppermute | solution.py:30
  213.8 41.0 %copy-start.17 = (bf16[1,256,512]{1,2,0:T(8,128)(2,1)}, bf16[1,256,512]{1,2,0:T(8,128)(2,1)S(1)}, u32[]{:S(2)}) copy-start(bf16[1,256,512]{1,2,0:T(8,128)(2,1)S(1)} %copy.1011) | copy-start | bytes 786436
  214.1 40.7 %copy-start.105 = (f32[4,128]{1,0:T(4,128)}, f32[4,128]{1,0:T(4,128)S(1)}, u32[]{:S(2)}) copy-start(f32[4,128]{1,0:T(4,128)S(1)} %get-tuple-element.92) | copy-start | bytes 6148
  258.2 7.8 copy-start.37
  258.2 7.8 copy-start.63
  262.9 15.2 %collective-permute-start.6 = (bf16[256,1024]{1,0:T(8,128)(2,1)}, bf16[256,1024]{1,0:T(8,128)(2,1)}, u32[]{:S(2)}, u32[]{:S(2)}) collective-permute-start(bf16[256,1024]{1,0:T(8,128)(2,1)} %bitcast.532), channel_id=1, source_target_pairs={{0,128},{8,136},{16,144},{24,152},{32,160},{40,168},{48,176},{56,1... | collective-permute-start | bytes 1572872 | tf_op jit(solution)/shard_map/ppermute | solution.py:30
  284.9 9.4 copy-start.78
  289.6 35.9 %collective-permute-start.7 = (bf16[256,1024]{1,0:T(8,128)(2,1)}, bf16[256,1024]{1,0:T(8,128)(2,1)}, u32[]{:S(2)}, u32[]{:S(2)}) collective-permute-start(bf16[256,1024]{1,0:T(8,128)(2,1)} %bitcast.531), channel_id=1, source_target_pairs={{0,256},{8,264},{16,272},{24,280},{32,288},{40,296},{48,304},{56,3... | collective-permute-start | bytes 1572872 | tf_op jit(solution)/shard_map/ppermute | solution.py:30
  418.8 14.8 %copy-start.104 = (pred[2,768]{1,0:T(4,128)(4,1)S(1)}, pred[2,768]{1,0:T(4,128)(4,1)}, u32[]{:S(2)}) copy-start(pred[2,768]{1,0:T(4,128)(4,1)} %copy-done.103) | copy-start | bytes 4612
  423.8 36.6 %copy-start.85 = (f32[4,256]{1,0:T(4,128)}, f32[4,256]{1,0:T(4,128)S(1)}, u32[]{:S(2)}) copy-start(f32[4,256]{1,0:T(4,128)S(1)} %copy.1041) | copy-start | bytes 12292
  438.1 6.4 copy-start.120
  457.9 6.7 copy-start.88
  480.2 10.2 %copy-start.98 = (f32[4,512]{1,0:T(4,128)}, f32[4,512]{1,0:T(4,128)S(1)}, u32[]{:S(2)}) copy-start(f32[4,512]{1,0:T(4,128)S(1)} %get-tuple-element.81) | copy-start | bytes 24580
  490.4 7.2 copy-start.11
  490.4 7.2 copy-start.27
  497.7 6.4 copy-start.96
  524.3 14.3 %copy-start.112 = (f32[4,512]{1,0:T(4,128)S(1)}, f32[4,512]{1,0:T(4,128)}, u32[]{:S(2)}) copy-start(f32[4,512]{1,0:T(4,128)} %get-tuple-element.75) | copy-start | bytes 24580
  524.3 386.1 %collective-permute-start.8 = (f32[256,1024]{1,0:T(8,128)}, f32[256,1024]{1,0:T(8,128)}, u32[]{:S(2)}, u32[]{:S(2)}) collective-permute-start(f32[256,1024]{1,0:T(8,128)} %get-tuple-element.32), channel_id=1, source_target_pairs={{0,8},{8,16},{16,24},{24,32},{32,40},{40,48},{48,56},{56,64},{64,7... | collective-permute-start | bytes 3145736 | tf_op jit(solution)/shard_map/ppermute | solution.py:23
  526.7 383.7 %collective-permute-start.9 = (f32[256,1024]{1,0:T(8,128)}, f32[256,1024]{1,0:T(8,128)}, u32[]{:S(2)}, u32[]{:S(2)}) collective-permute-start(f32[256,1024]{1,0:T(8,128)} %get-tuple-element.33), channel_id=1, source_target_pairs={{8,0},{16,8},{24,16},{32,24},{40,32},{48,40},{56,48},{64,56},{72,6... | collective-permute-start | bytes 3145736 | tf_op jit(solution)/shard_map/ppermute | solution.py:24
  531.1 10.7 %copy-start.92 = (f32[4,32]{1,0:T(4,128)S(1)}, f32[4,32]{1,0:T(4,128)}, u32[]{:S(2)}) copy-start(f32[4,32]{1,0:T(4,128)} %copy.1073) | copy-start | bytes 1540
  543.1 14.4 %copy-start.81 = (bf16[16,512]{1,0:T(8,128)(2,1)S(1)}, bf16[16,512]{1,0:T(8,128)(2,1)}, u32[]{:S(2)}) copy-start(bf16[16,512]{1,0:T(8,128)(2,1)} %get-tuple-element.24) | copy-start | bytes 49156
  564.6 10.0 %copy-start.79 = (f32[8,1,512]{2,1,0:T(1,128)S(1)}, f32[8,1,512]{2,1,0:T(1,128)}, u32[]{:S(2)}) copy-start(f32[8,1,512]{2,1,0:T(1,128)} %get-tuple-element.68) | copy-start | bytes 49156
  575.8 14.1 %copy-start.93 = (f32[4,32]{1,0:T(4,128)S(1)}, f32[4,32]{1,0:T(4,128)}, u32[]{:S(2)}) copy-start(f32[4,32]{1,0:T(4,128)} %copy.1073) | copy-start | bytes 1540
  578.8 18.1 %copy-start.32 = (bf16[1,256,512]{1,2,0:T(8,128)(2,1)S(1)}, bf16[1,256,512]{1,2,0:T(8,128)(2,1)}, u32[]{:S(2)}) copy-start(bf16[1,256,512]{1,2,0:T(8,128)(2,1)} %copy.1054) | copy-start | bytes 786436
  578.8 18.1 %copy-start.91 = (f32[4,64]{1,0:T(4,128)S(1)}, f32[4,64]{1,0:T(4,128)}, u32[]{:S(2)}) copy-start(f32[4,64]{1,0:T(4,128)} %copy.1062) | copy-start | bytes 3076
  581.1 16.7 %copy-start.29 = (f32[128,4,128]{0,2,1:T(8,128)S(1)}, f32[128,4,128]{0,2,1:T(8,128)}, u32[]{:S(2)}) copy-start(f32[128,4,128]{0,2,1:T(8,128)} %copy.1175) | copy-start | bytes 786436
  581.1 16.7 %copy-start.89 = (f32[4,128]{1,0:T(4,128)S(1)}, f32[4,128]{1,0:T(4,128)}, u32[]{:S(2)}) copy-start(f32[4,128]{1,0:T(4,128)} %copy-done.87) | copy-start | bytes 6148
  581.1 27.7 %collective-permute-start.10 = (f32[256,1024]{1,0:T(8,128)}, f32[256,1024]{1,0:T(8,128)}, u32[]{:S(2)}, u32[]{:S(2)}) collective-permute-start(f32[256,1024]{1,0:T(8,128)} %maximum_bitcast_fusion), channel_id=1, source_target_pairs={{0,256},{8,264},{16,272},{24,280},{32,288},{40,296},{48,304},{56,3... | collective-permute-start | bytes 3145736 | tf_op jit(solution)/shard_map/ppermute | solution.py:30
  596.9 13.3 %copy-start.56 = (f32[64,4,128]{2,1,0:T(4,128)}, f32[64,4,128]{2,1,0:T(4,128)S(1)}, u32[]{:S(2)}) copy-start(f32[64,4,128]{2,1,0:T(4,128)S(1)} %multiply_reduce_fusion.3) | copy-start | bytes 393220
  598.3 27.9 %copy-start.15 = (bf16[4,128,256]{2,1,0:T(8,128)(2,1)}, bf16[4,128,256]{2,1,0:T(8,128)(2,1)S(1)}, u32[]{:S(2)}) copy-start(bf16[4,128,256]{2,1,0:T(8,128)(2,1)S(1)} %fusion.19) | copy-start | bytes 786436
  614.3 7.3 copy-start.65
  614.3 7.3 copy-start.76
  616.7 9.5 copy-start.51
  616.7 25.7 %collective-permute-start.11 = (f32[256,1024]{1,0:T(8,128)}, f32[256,1024]{1,0:T(8,128)}, u32[]{:S(2)}, u32[]{:S(2)}) collective-permute-start(f32[256,1024]{1,0:T(8,128)} %fusion.46), channel_id=1, source_target_pairs={{0,128},{8,136},{16,144},{24,152},{32,160},{40,168},{48,176},{56,1... | collective-permute-start | bytes 3145736 | tf_op jit(solution)/shard_map/ppermute | solution.py:30
  648.0 7.8 copy-start.57
  648.0 7.8 copy-start.64
  648.0 10.9 %copy-start.47 = (f32[4,128,256]{2,1,0:T(8,128)S(1)}, f32[4,128,256]{2,1,0:T(8,128)}, u32[]{:S(2)}) copy-start(f32[4,128,256]{2,1,0:T(8,128)} %fusion.97) | copy-start | bytes 1572868
  650.4 71.5 %collective-permute-start.12 = (f32[256,1024]{1,0:T(8,128)}, f32[256,1024]{1,0:T(8,128)}, u32[]{:S(2)}, u32[]{:S(2)}) collective-permute-start(f32[256,1024]{1,0:T(8,128)} %fusion.47), channel_id=1, source_target_pairs={{0,64},{8,72},{16,80},{24,88},{32,96},{40,104},{48,112},{56,120},{... | collective-permute-start | bytes 3145736 | tf_op jit(solution)/shard_map/ppermute | solution.py:30
  656.8 7.3 copy-start.48
  727.7 88.6 %collective-permute-start.13 = (f32[256,1024]{1,0:T(8,128)}, f32[256,1024]{1,0:T(8,128)}, u32[]{:S(2)}, u32[]{:S(2)}) collective-permute-start(f32[256,1024]{1,0:T(8,128)} %fusion.48), channel_id=1, source_target_pairs={{0,32},{8,40},{16,48},{24,56},{32,0},{40,8},{48,16},{56,24},{64,96... | collective-permute-start | bytes 3145736 | tf_op jit(solution)/shard_map/ppermute | solution.py:30
  822.1 46.0 %collective-permute-start.14 = (f32[256,1024]{1,0:T(8,128)}, f32[256,1024]{1,0:T(8,128)}, u32[]{:S(2)}, u32[]{:S(2)}) collective-permute-start(f32[256,1024]{1,0:T(8,128)} %fusion.49), channel_id=1, source_target_pairs={{0,16},{8,24},{16,0},{24,8},{32,48},{40,56},{48,32},{56,40},{64,80... | collective-permute-start | bytes 3145736 | tf_op jit(solution)/shard_map/ppermute | solution.py:30
  874.1 40.7 %collective-permute-start.15 = (f32[256,1024]{1,0:T(8,128)}, f32[256,1024]{1,0:T(8,128)}, u32[]{:S(2)}, u32[]{:S(2)}) collective-permute-start(f32[256,1024]{1,0:T(8,128)} %fusion.50), channel_id=1, source_target_pairs={{0,8},{8,0},{16,24},{24,16},{32,40},{40,32},{48,56},{56,48},{64,72... | collective-permute-start | bytes 3145736 | tf_op jit(solution)/shard_map/ppermute | solution.py:30
  877.5 6.4 copy-start.9
  877.6 43.4 %all-to-all-start.5 = ((bf16[8,64,512]{2,1,0:T(8,128)(2,1)}), bf16[8,64,512]{2,1,0:T(8,128)(2,1)}, u32[]{:S(2)}, u32[]{:S(2)}) async-start(bf16[8,64,512]{2,1,0:T(8,128)(2,1)} %add_convert_fusion), calls=%async_computation.5 | async-start | bytes 1048576 | tf_op jit(solution)/shard_map/all_to_all | solution.py:267
  903.8 6.6 copy-start.3
  921.0 14.3 %all-to-all-start.3 = ((bf16[8,64,512]{2,1,0:T(8,128)(2,1)}), bf16[8,64,512]{2,1,0:T(8,128)(2,1)}, u32[]{:S(2)}, u32[]{:S(2)}) async-start(bf16[8,64,512]{2,1,0:T(8,128)(2,1)} %divide_convert_fusion), calls=%async_computation.3 | async-start | bytes 1048576 | tf_op jit(solution)/shard_map/all_to_all | solution.py:266
  948.0 13.8 %all-to-all-start.7 = ((bf16[8,64,512]{2,1,0:T(8,128)(2,1)}), bf16[8,64,512]{2,1,0:T(8,128)(2,1)S(1)}, u32[]{:S(2)}, u32[]{:S(2)}) async-start(bf16[8,64,512]{2,1,0:T(8,128)(2,1)} %bitcast.202), calls=%async_computation.7 | async-start | bytes 1048576 | tf_op jit(solution)/shard_map/all_to_all | solution.py:269
  (81 other events, 257.9 us)
where the time goes:
time: 979 us; the launch traced here: 963 us
  local copies, waits for them, and re-layouts  346 us (35%)
  waiting for transfers between devices  293 us (30%)
  other arithmetic  144 us (15%)
  starting transfers between devices  101 us (10%)
  matrix products  64.3 us (7%)
  blocking collectives  12.7 us (1%)
    ppermute x12, waiting for transfers between devices, partner(): lax.ppermute(array, axis, [(i, i ^ 1 << distance) for i in range(lax.axis...  259 us
    ppermute x12, starting transfers between devices, partner(): lax.ppermute(array, axis, [(i, i ^ 1 << distance) for i in range(lax.axis...  55.8 us
    broadcast_in_dim x41, local copies, waits for them, and re-layouts, per_device(): jnp.repeat(to_heads(jnp.max(coarse_scores, axis=3)), 2 ** height, axis=1)  33.6 us
    convert_element_type x11, other arithmetic, coarsen(): return ((paired[:, 0] + paired[:, 1]) * 0.5).astype(jnp.bfloat16)  23.4 us
    slice x12, local copies, waits for them, and re-layouts, per_device(): pair_blk[:, :, features:].reshape(groups, block_rows, head_count, head_dim)  20.8 us
    convert_element_type x11, local copies, waits for them, and re-layouts, coarsen(): matrix.reshape(matrix.shape[0] // 2, 2, matrix.shape[1]).astype(jnp.float32)  19.7 us
  transfers between devices with their start and end apart: 23, of which 15 were waited for; matrix products, arithmetic and copies ran while one was open for 32% of the time, Pallas kernels for 0%

commit v1 on v0

v1 whole, which is shorter than its diff:
```python
import math

import jax
import jax.numpy as jnp
from jax import lax
from jax.experimental import pallas as pl
from jax.experimental.pallas import tpu as pltpu
from jax.sharding import Mesh, PartitionSpec as P

HD = 128
BLOCK = 256
LEVELS = 6
NEAR = 3 * BLOCK
SCALE = 1.0 / math.sqrt(HD)
FILL = -1e30
f32 = jnp.float32
bf16 = jnp.bfloat16

ROWS = 2048
CHUNK_BLOCKS = ROWS // BLOCK
COUNT = [ROWS >> l for l in range(LEVELS + 1)]
OFF = [0, 0, 1024, 1536, 1792, 1920, 1984]
COARSE_ROWS = 2016
SIB = [0, 0, 1024, 1536, 1792, 2048, 2304]
SIB_ROWS = 2560

VMEM = pl.BlockSpec(memory_space=pltpu.VMEM)
SMEM = pl.BlockSpec(memory_space=pltpu.SMEM)


def nn(a, b):
    return lax.dot_general(a, b, (((1,), (0,)), ((), ())), preferred_element_type=f32)


def nt(a, b):
    return lax.dot_general(a, b, (((1,), (1,)), ((), ())), preferred_element_type=f32)


def tn(a, b):
    return lax.dot_general(a, b, (((0,), (0,)), ((), ())), preferred_element_type=f32)


def tile(x, n):
    return jnp.concatenate([x] * n, axis=1)


def spread(x):
    return jnp.broadcast_to(x, (x.shape[0], HD))


def pooler(n):
    row = lax.broadcasted_iota(jnp.int32, (n, 2 * n), 0)
    col = lax.broadcasted_iota(jnp.int32, (n, 2 * n), 1)
    return jnp.where(col // 2 == row, 0.5, 0.0).astype(bf16)


def coarsen(x):
    return nn(pooler(x.shape[0] // 2), x).astype(bf16)


def rep(x, tmp):
    n = x.shape[0]
    tmp[pl.ds(0, n, stride=2), :] = x
    tmp[pl.ds(1, n, stride=2), :] = x
    return tmp[0 : 2 * n, :]


def rep_pair(x, tmp_a, tmp_b):
    return jnp.concatenate([rep(x[:, :HD], tmp_a), rep(x[:, HD:], tmp_b)], axis=1)


def pair_sum(x, tmp):
    n = x.shape[0] // 2
    tmp[0 : 2 * n, :] = x
    return tmp[pl.ds(0, n, stride=2), :] + tmp[pl.ds(1, n, stride=2), :]


def pack_kernel(a_ref, b_ref, o_ref):
    for h in range(o_ref.shape[0]):
        o_ref[h, :, 0:HD] = a_ref[:, h * HD : (h + 1) * HD]
        o_ref[h, :, HD : 2 * HD] = b_ref[:, h * HD : (h + 1) * HD]


def unpack_kernel(x_ref, a_ref, b_ref):
    for h in range(x_ref.shape[0]):
        a_ref[:, h * HD : (h + 1) * HD] = x_ref[h, :, 0:HD]
        b_ref[:, h * HD : (h + 1) * HD] = x_ref[h, :, HD : 2 * HD]


def levels_kernel(kv_ref, l1_ref, l2_ref, l4_ref, up_ref, down_ref):
    half = BLOCK // 2
    for b in range(8):
        l1_ref[b * half : (b + 1) * half, :] = coarsen(kv_ref[b * BLOCK : (b + 1) * BLOCK, :])
    for b in range(4):
        l2_ref[b * half : (b + 1) * half, :] = coarsen(l1_ref[b * BLOCK : (b + 1) * BLOCK, :])
    for b in range(2):
        l3 = coarsen(l2_ref[b * BLOCK : (b + 1) * BLOCK, :])
        up_ref[BLOCK + b * half : BLOCK + (b + 1) * half, :] = l3
        down_ref[BLOCK + b * half : BLOCK + (b + 1) * half, :] = l3
    l4_ref[...] = coarsen(up_ref[BLOCK : 2 * BLOCK, :])
    up_ref[0:BLOCK, :] = kv_ref[ROWS - BLOCK : ROWS, :]
    down_ref[0:BLOCK, :] = kv_ref[0:BLOCK, :]


def group_kernel(c_ref, l4_ref, before_ref, after_ref, z2_ref, z3_ref, g5_ref, g6_ref):
    even = c_ref[0] % 2 == 0
    l3 = jnp.where(even, after_ref[BLOCK : 2 * BLOCK, :], before_ref[BLOCK : 2 * BLOCK, :])
    g5_ref[0:64, :] = coarsen(l4_ref[...])
    g5_ref[64:128, :] = coarsen(coarsen(l3))
    g5_ref[128:192, :] = coarsen(z2_ref[...])
    g5_ref[192:256, :] = coarsen(z3_ref[...])
    g6_ref[...] = coarsen(g5_ref[...])


def main_kernel(
    c_ref, kv_ref, qg_ref, l1_ref, l2_ref, before_ref, after_ref, z2_ref, z3_ref, y1_ref, y2_ref, y3_ref,
    ag_ref, d_ref, ups_ref, downs_ref, g3_ref, g4_ref, t1_ref, t2_ref, t3_ref,
    kx, gkx, qc, sib, gs, w_s, u_s, s_s, acc_s, e_s, po_s, pd_s, gq_s, gq0, tmp,
):
    c = c_ref[0]
    half = BLOCK // 2
    even = c % 2 == 0

    kx[0:BLOCK, :] = before_ref[0:BLOCK, :]
    kx[BLOCK : BLOCK + ROWS, :] = kv_ref[...]
    kx[BLOCK + ROWS :, :] = after_ref[0:BLOCK, :]
    gkx[...] = jnp.zeros_like(gkx)
    for b in range(4):
        sib[SIB[1] + b * BLOCK : SIB[1] + (b + 1) * BLOCK, :] = l1_ref[(b ^ 1) * BLOCK : ((b ^ 1) + 1) * BLOCK, :]
    for b in range(2):
        sib[SIB[2] + b * BLOCK : SIB[2] + (b + 1) * BLOCK, :] = l2_ref[(b ^ 1) * BLOCK : ((b ^ 1) + 1) * BLOCK, :]
    sib[SIB[3] : SIB[3] + BLOCK, :] = jnp.where(
        even, after_ref[BLOCK : 2 * BLOCK, :], before_ref[BLOCK : 2 * BLOCK, :]
    )
    sib[SIB[4] : SIB[4] + half, :] = z2_ref[...]
    sib[SIB[4] + half : SIB[4] + BLOCK, :] = z3_ref[...]
    sib[SIB[5] : SIB[5] + BLOCK, :] = y1_ref[...]
    sib[SIB[6] : SIB[6] + half, :] = y2_ref[...]
    sib[SIB[6] + half : SIB[6] + BLOCK, :] = y3_ref[...]

    for b in range(8):
        qc[b * half : (b + 1) * half, :] = coarsen(qg_ref[b * BLOCK : (b + 1) * BLOCK, 0:HD])
    for l in range(2, LEVELS + 1):
        n = min(COUNT[l], half)
        for b in range(COUNT[l] // n):
            src = OFF[l - 1] + 2 * b * n
            qc[OFF[l] + b * n : OFF[l] + (b + 1) * n, :] = coarsen(qc[src : src + 2 * n, :])

    def level_down(l, r0, n, s0, p0):
        rows = pl.ds(r0, n)
        kvs = sib[pl.ds(s0, BLOCK), :]
        scores = nt(qc[rows, :], kvs[:, :HD]) * SCALE
        u = spread(jnp.max(scores, axis=1, keepdims=True))
        if l < LEVELS:
            parent = pl.ds(p0, n // 2)
            pu = rep(u_s[parent, :], tmp.at[0])
            u = jnp.maximum(u, pu)
            e = jnp.exp(pu - u)
            e_s[rows, :] = e
        weights = jnp.exp(scores - tile(u, 2)) * (2.0**l)
        total = spread(jnp.sum(weights, axis=1, keepdims=True))
        acc = nn(weights.astype(bf16), kvs[:, HD:])
        if l < LEVELS:
            total = total + e * rep(s_s[parent, :], tmp.at[1])
            acc = acc + e * rep(acc_s[parent, :], tmp.at[2])
        w_s[rows, :] = weights
        u_s[rows, :] = u
        s_s[rows, :] = total
        acc_s[rows, :] = acc

    def level_up(l, r0, n, s0, p0):
        rows = pl.ds(r0, n)
        kvs = sib[pl.ds(s0, BLOCK), :]
        po = po_s[rows, :]
        pd = pd_s[rows, :]
        high = po.astype(bf16)
        low = (po - high.astype(f32)).astype(bf16)
        parts = jnp.concatenate([high, low], axis=1)
        prod = nt(parts, tile(kvs[:, HD:], 2))
        weights = w_s[rows, :]
        grads = (weights * (prod - tile(pd, 2)) * SCALE).astype(bf16)
        gq_s[rows, :] = nn(grads, kvs[:, :HD])
        gs[pl.ds(s0, BLOCK), 0:HD] = tn(grads, qc[rows, :])
        gv = tn(weights.astype(bf16), parts)
        gs[pl.ds(s0, BLOCK), HD : 2 * HD] = gv[:, :HD] + gv[:, HD:]
        if l < LEVELS:
            e = e_s[rows, :]
            parent = pl.ds(p0, n // 2)
            po_s[parent, :] = pair_sum(e * po, tmp.at[0])
            pd_s[parent, :] = pair_sum(e * pd, tmp.at[1])

    def each_block(step, l):
        def body(b, carry):
            step(
                l,
                pl.multiple_of(OFF[l] + b * BLOCK, BLOCK),
                BLOCK,
                pl.multiple_of(SIB[l] + b * BLOCK, BLOCK),
                pl.multiple_of(OFF[l + 1] + b * half, half),
            )
            return carry

        lax.fori_loop(0, COUNT[l] // BLOCK, body, 0)

    for l in range(LEVELS, 2, -1):
        level_down(l, OFF[l], COUNT[l], SIB[l], OFF[l + 1] if l < LEVELS else 0)
    each_block(level_down, 2)
    each_block(level_down, 1)

    def near(b, carry):
        r = pl.multiple_of(b * BLOCK, BLOCK)
        rows = pl.ds(r, BLOCK)
        window = pl.ds(r, NEAR)
        coarse = pl.ds(pl.multiple_of(b * half, half), half)
        q = qg_ref[rows, 0:HD]
        g = qg_ref[rows, HD : 2 * HD]
        k_win = kx[window, 0:HD]
        v_win = kx[window, HD : 2 * HD]
        column = lax.broadcasted_iota(jnp.int32, (1, NEAR), 1)
        first = jnp.logical_and(c == 0, b == 0)
        last = jnp.logical_and(c == 15, b == CHUNK_BLOCKS - 1)
        low = jnp.where(first, BLOCK, 0)
        high = jnp.where(last, 2 * BLOCK, NEAR)
        bias = jnp.where(jnp.logical_and(column >= low, column < high), 0.0, FILL)
        scores = nt(q, k_win) * SCALE + bias
        pu = rep(u_s[coarse, :], tmp.at[0])
        m = jnp.maximum(spread(jnp.max(scores, axis=1, keepdims=True)), pu)
        e = jnp.exp(pu - m)
        weights = jnp.exp(scores - tile(m, 6))
        totals = spread(jnp.sum(weights, axis=1, keepdims=True)) + e * rep(s_s[coarse, :], tmp.at[1])
        numerator = nn(weights.astype(bf16), v_win) + e * rep(acc_s[coarse, :], tmp.at[2])
        inverse = 1.0 / totals
        attended = numerator * inverse
        ag_ref[rows, 0:HD] = attended.astype(bf16)
        gf = g.astype(f32)
        delta = spread(jnp.sum(gf * attended, axis=1, keepdims=True))
        shares = weights * tile(inverse, 6)
        prod = nt(g, v_win)
        grads = (shares * (prod - tile(delta, 6)) * SCALE).astype(bf16)
        gq0[rows, :] = nn(grads, k_win)
        gkx[window, 0:HD] += tn(grads, q)
        gkx[window, HD : 2 * HD] += tn(shares.astype(bf16), g)
        scaled = e * inverse
        po_s[coarse, :] = pair_sum(scaled * gf, tmp.at[3])
        pd_s[coarse, :] = pair_sum(scaled * delta, tmp.at[4])
        return carry

    lax.fori_loop(0, CHUNK_BLOCKS, near, 0)

    each_block(level_up, 1)
    each_block(level_up, 2)
    for l in range(3, LEVELS + 1):
        level_up(l, OFF[l], COUNT[l], SIB[l], OFF[l + 1] if l < LEVELS else 0)

    for l in range(LEVELS - 1, 0, -1):
        n = min(COUNT[l], BLOCK)
        for b in range(COUNT[l] // n):
            src = OFF[l + 1] + b * (n // 2)
            rows = slice(OFF[l] + b * n, OFF[l] + (b + 1) * n)
            gq_s[rows, :] += rep(gq_s[src : src + n // 2, :] * 0.5, tmp.at[b % 5])
    for j in range(4):
        own = gs.at[SIB[1] + (j ^ 1) * BLOCK : SIB[1] + ((j ^ 1) + 1) * BLOCK]
        i = j // 2
        above = SIB[2] + (i ^ 1) * BLOCK + (j % 2) * half
        own[...] += rep_pair(gs[above : above + half, :] * 0.5, tmp.at[0], tmp.at[1])

    def finish(b, carry):
        rows = pl.ds(pl.multiple_of(b * BLOCK, BLOCK), BLOCK)
        coarse = pl.ds(pl.multiple_of(b * half, half), half)
        ag_ref[rows, HD : 2 * HD] = (gq0[rows, :] + rep(gq_s[coarse, :] * 0.5, tmp.at[0])).astype(bf16)
        j = b // 2
        src = pl.multiple_of(SIB[1] + (j + 1 - 2 * (j % 2)) * BLOCK + (b % 2) * half, half)
        own = pl.ds(pl.multiple_of((b + 1) * BLOCK, BLOCK), BLOCK)
        d_ref[rows, :] = gkx[own, :] + rep_pair(gs[pl.ds(src, half), :] * 0.5, tmp.at[1], tmp.at[2])
        return carry

    lax.fori_loop(0, CHUNK_BLOCKS, finish, 0)
    downs_ref[...] = gkx[0:BLOCK, :].astype(bf16)
    ups_ref[...] = gkx[BLOCK + ROWS :, :].astype(bf16)
    g3_ref[...] = gs[SIB[3] : SIB[3] + BLOCK, :]
    g4_ref[...] = gs[SIB[4] : SIB[4] + BLOCK, :]
    t1_ref[...] = gs[SIB[5] : SIB[5] + BLOCK, :].astype(bf16)
    t2_ref[...] = gs[SIB[6] : SIB[6] + half, :].astype(bf16)
    t3_ref[...] = gs[SIB[6] + half : SIB[6] + BLOCK, :].astype(bf16)


def fold_kernel(
    ups_ref, downs_ref, g3_ref, g4_ref, r1_ref, r2_ref, r3_ref, up_ref, down_ref, z2_ref, z3_ref, own_ref, tmp
):
    def rep2(x):
        return rep_pair(x * 0.5, tmp.at[0], tmp.at[1])

    g6 = r2_ref[...].astype(f32) + r3_ref[...].astype(f32)
    g5 = r1_ref[...].astype(f32) + rep2(g6)
    own_ref[...] = g5[0:64, :]
    l3 = (g3_ref[...] + rep2(rep2(g5[64:128, :]))).astype(bf16)
    up_ref[0:BLOCK, :] = ups_ref[...]
    up_ref[BLOCK : 2 * BLOCK, :] = l3
    down_ref[0:BLOCK, :] = downs_ref[...]
    down_ref[BLOCK : 2 * BLOCK, :] = l3
    z2_ref[...] = (g4_ref[0:128, :] + rep2(g5[128:192, :])).astype(bf16)
    z3_ref[...] = (g4_ref[128:256, :] + rep2(g5[192:256, :])).astype(bf16)


def combine_kernel(c_ref, d_ref, before_ref, after_ref, z2_ref, z3_ref, own_ref, o_ref, tmp, a_s, b_s):
    even = c_ref[0] % 2 == 0

    def rep2(x):
        return rep_pair(x * 0.5, tmp.at[0], tmp.at[1])

    l3 = jnp.where(even, after_ref[BLOCK : 2 * BLOCK, :], before_ref[BLOCK : 2 * BLOCK, :])
    g4 = z2_ref[...].astype(f32) + z3_ref[...].astype(f32) + rep2(own_ref[...])
    g3 = l3.astype(f32) + rep2(g4)
    half = BLOCK // 2
    for b in range(2):
        a_s[b * BLOCK : (b + 1) * BLOCK, :] = rep2(g3[b * half : (b + 1) * half, :])
    for b in range(4):
        b_s[b * BLOCK : (b + 1) * BLOCK, :] = rep2(a_s[b * half : (b + 1) * half, :])
    for b in range(8):
        total = d_ref[b * BLOCK : (b + 1) * BLOCK, :] + rep2(b_s[b * half : (b + 1) * half, :])
        if b == 0:
            total = total + before_ref[0:BLOCK, :].astype(f32)
        if b == 7:
            total = total + after_ref[0:BLOCK, :].astype(f32)
        o_ref[b * BLOCK : (b + 1) * BLOCK, :] = total.astype(bf16)


def shape(dtype, *dims):
    return jax.ShapeDtypeStruct(dims, dtype)


def call(kernel, name, out_shape, scalars, args, scratch=(), flops=0):
    nbytes = sum(a.size * a.dtype.itemsize for a in args)
    return pl.pallas_call(
        kernel,
        name=name,
        out_shape=out_shape,
        in_specs=[SMEM] * scalars + [VMEM] * (len(args) - scalars),
        out_specs=jax.tree.map(lambda _: VMEM, out_shape),
        scratch_shapes=list(scratch),
        cost_estimate=pl.CostEstimate(flops=flops, bytes_accessed=2 * nbytes, transcendentals=0),
    )(*args)


def per_device(queries, key_rows, value_rows, cotangent):
    own_rows, width = queries.shape
    heads = width // HD
    peers = heads
    chunk = (lax.axis_index("y") * lax.axis_size("zh") + lax.axis_index("zh")).astype(jnp.int32).reshape(1)

    def pack(a, b, name):
        return call(pack_kernel, name, shape(bf16, heads, own_rows, 2 * HD), 0, (a, b))

    def swap(x):
        return lax.all_to_all(x, ("zl", "h"), split_axis=0, concat_axis=0, tiled=True)

    def shift(x, distance):
        pairs = [(i, i + distance) for i in range(16) if 0 <= i + distance < 16]
        return lax.ppermute(x, ("y", "zh"), pairs)

    def flip(x, axis, bits):
        return lax.ppermute(x, axis, [(i, i ^ bits) for i in range(4)])

    kv = swap(pack(key_rows, value_rows, "pack_kv")).reshape(ROWS, 2 * HD)
    l1, l2, l4, up, down = call(
        levels_kernel,
        "levels",
        (
            shape(bf16, 1024, 2 * HD),
            shape(bf16, 512, 2 * HD),
            shape(bf16, 128, 2 * HD),
            shape(bf16, 2 * BLOCK, 2 * HD),
            shape(bf16, 2 * BLOCK, 2 * HD),
        ),
        0,
        (kv,),
    )
    before, after = shift(up, 1), shift(down, -1)
    z2, z3 = flip(l4, "zh", 2), flip(l4, "zh", 3)
    packed = pack(queries, cotangent, "pack_qg")
    qg = swap(packed).reshape(ROWS, 2 * HD)
    g5, g6 = call(
        group_kernel,
        "group",
        (shape(bf16, BLOCK, 2 * HD), shape(bf16, 128, 2 * HD)),
        1,
        (chunk, l4, before, after, z2, z3),
    )
    y1, y2, y3 = flip(g5, "y", 1), flip(g6, "y", 2), flip(g6, "y", 3)
    coarse = pltpu.VMEM((COARSE_ROWS, HD), f32)
    ag, d, ups, downs, g3, g4, t1, t2, t3 = call(
        main_kernel,
        "attend",
        (
            shape(bf16, ROWS, 2 * HD),
            shape(f32, ROWS, 2 * HD),
            shape(bf16, BLOCK, 2 * HD),
            shape(bf16, BLOCK, 2 * HD),
            shape(f32, BLOCK, 2 * HD),
            shape(f32, BLOCK, 2 * HD),
            shape(bf16, BLOCK, 2 * HD),
            shape(bf16, 128, 2 * HD),
            shape(bf16, 128, 2 * HD),
        ),
        1,
        (chunk, kv, qg, l1, l2, before, after, z2, z3, y1, y2, y3),
        scratch=(
            pltpu.VMEM((ROWS + 2 * BLOCK, 2 * HD), bf16),
            pltpu.VMEM((ROWS + 2 * BLOCK, 2 * HD), f32),
            pltpu.VMEM((COARSE_ROWS, HD), bf16),
            pltpu.VMEM((SIB_ROWS, 2 * HD), bf16),
            pltpu.VMEM((SIB_ROWS, 2 * HD), f32),
            pltpu.VMEM((COARSE_ROWS, 2 * HD), f32),
            coarse,
            coarse,
            coarse,
            coarse,
            coarse,
            coarse,
            coarse,
            pltpu.VMEM((ROWS, HD), f32),
            pltpu.VMEM((5, BLOCK, HD), f32),
        ),
        flops=4_000_000_000,
    )
    out_ag = swap(ag.reshape(peers, own_rows, 2 * HD))
    r1, r2, r3 = flip(t1, "y", 1), flip(t2, "y", 2), flip(t3, "y", 3)
    up, down, z2, z3, own5 = call(
        fold_kernel,
        "fold",
        (
            shape(bf16, 2 * BLOCK, 2 * HD),
            shape(bf16, 2 * BLOCK, 2 * HD),
            shape(bf16, 128, 2 * HD),
            shape(bf16, 128, 2 * HD),
            shape(f32, 64, 2 * HD),
        ),
        0,
        (ups, downs, g3, g4, r1, r2, r3),
        scratch=(pltpu.VMEM((2, BLOCK, HD), f32),),
    )
    before, after = shift(up, 1), shift(down, -1)
    z2, z3 = flip(z2, "zh", 2), flip(z3, "zh", 3)
    gkv = call(
        combine_kernel,
        "combine",
        shape(bf16, ROWS, 2 * HD),
        1,
        (chunk, d, before, after, z2, z3, own5),
        scratch=(
            pltpu.VMEM((2, BLOCK, HD), f32),
            pltpu.VMEM((512, 2 * HD), f32),
            pltpu.VMEM((1024, 2 * HD), f32),
        ),
    )
    out_kv = swap(gkv.reshape(peers, own_rows, 2 * HD))
    pair = (shape(bf16, own_rows, width), shape(bf16, own_rows, width))
    attended, grad_query = call(unpack_kernel, "unpack_ag", pair, 0, (out_ag,))
    grad_key, grad_value = call(unpack_kernel, "unpack_kv", pair, 0, (out_kv,))
    return attended, grad_query, grad_key, grad_value


def solution(mesh):
    grid = Mesh(mesh.devices.reshape(4, 4, 4, 8), ("y", "zh", "zl", "h"))
    spec = P(("y", "zh", "zl", "h"), None)
    return jax.shard_map(
        per_device,
        mesh=grid,
        in_specs=(spec,) * 4,
        out_specs=(spec,) * 4,
        check_vma=False,
    )
```

time: 979 us -> 260 us (0.27); the launches traced: 963 us -> 259 us
  local copies, waits for them, and re-layouts: 346 us -> 3.86 us
  waiting for transfers between devices: 293 us -> 100 us
  other arithmetic: 144 us -> 0 us
  matrix products: 64.3 us -> 0 us
  Pallas kernels: 0 us -> 44.3 us
  blocking collectives: 12.7 us -> 0 us
    ppermute x16 -> x14, waiting for transfers between devices: 259 us -> 51.9 us  [the longest x10 45.9 us: flip(): return lax.ppermute(x, axis, [(i, i ^ bits) for i in range(4)])]
    reshape x84 -> x0, local copies, waits for them, and re-layouts: 114 us -> none  [the longest x12 18.7 us: per_device(): jnp.repeat(to_heads(jnp.sum(coarse_weights, axis=3)), repeat, axis=1)]
    dot_general x42 -> x0, matrix products: 64.3 us -> none  [the longest x6 9.63 us: per_device(): jnp.einsum('ghrj,grhd->gjhd', rounded_coarse.astype(jnp.float32), pooled_...]
    broadcast_in_dim x75 -> x0, local copies, waits for them, and re-layouts: 58.8 us -> none  [the longest x41 33.6 us: per_device(): jnp.repeat(to_heads(jnp.max(coarse_scores, axis=3)), 2 ** height, axis=1)]
    convert_element_type x24 -> x0, other arithmetic: 50.5 us -> none  [the longest x11 23.4 us: coarsen(): return ((paired[:, 0] + paired[:, 1]) * 0.5).astype(jnp.bfloat16)]
    pallas_call x0 -> x9, Pallas kernels: none -> 44.3 us  [call(): pl.pallas_call(kernel, name=name, out_shape=out_shape, in_specs=[SMEM] *...]
    slice x25 -> x0, local copies, waits for them, and re-layouts: 38.1 us -> none  [the longest x12 20.8 us: per_device(): pair_blk[:, :, features:].reshape(groups, block_rows, head_count, head_dim)]
    convert_element_type x18 -> x0, local copies, waits for them, and re-layouts: 28.2 us -> none  [the longest x11 19.7 us: coarsen(): matrix.reshape(matrix.shape[0] // 2, 2, matrix.shape[1]).astype(jnp.float32)]
  transfers between devices with their start and end apart: 23 -> 18, of which waited for: 15 -> 9; matrix products, arithmetic and copies ran while one was open for 32% -> 0% of each run, Pallas kernels for 0% -> 6%
where the time goes in v1:
time: 260 us; the launch traced here: 259 us
  starting transfers between devices  109 us (42%)
  waiting for transfers between devices  100 us (38%)
  Pallas kernels  44.3 us (17%)
  local copies, waits for them, and re-layouts  3.86 us (1%)
    all_to_all x4, waiting for transfers between devices, swap(): lax.all_to_all(x, ('zl', 'h'), split_axis=0, concat_axis=0, tiled=True)  48.6 us
    ppermute x10, starting transfers between devices, flip(): return lax.ppermute(x, axis, [(i, i ^ bits) for i in range(4)])  48.3 us
    ppermute x10, waiting for transfers between devices, flip(): return lax.ppermute(x, axis, [(i, i ^ bits) for i in range(4)])  45.9 us
    pallas_call x9, Pallas kernels, call(): pl.pallas_call(kernel, name=name, out_shape=out_shape, in_specs=[SMEM] *...  44.3 us
    all_to_all x4, starting transfers between devices, swap(): lax.all_to_all(x, ('zl', 'h'), split_axis=0, concat_axis=0, tiled=True)  43.6 us
    ppermute x4, starting transfers between devices, shift(): return lax.ppermute(x, ('y', 'zh'), pairs)  17.1 us
    ppermute x4, waiting for transfers between devices, shift(): return lax.ppermute(x, ('y', 'zh'), pairs)  5.99 us
  transfers between devices with their start and end apart: 18, of which 9 were waited for; matrix products, arithmetic and copies ran while one was open for 0% of the time, Pallas kernels for 6%

profile of v1, /device:TPU:1, one launch (start us, length us, event | category | flops | bytes accessed | tf_op | source)
XLA Modules:
  0.0 258.5 jit_solution(6772014582713417570)
XLA Ops:
  0.6 2.4 pack_kv.1
  3.0 10.4 %all-to-all-start = ((bf16[32,64,256]{2,1,0:T(8,128)(2,1)}), bf16[32,64,256]{2,1,0:T(8,128)(2,1)S(1)}, u32[]{:S(2)}, u32[]{:S(2)}) async-start(bf16[32,64,256]{2,1,0:T(8,128)(2,1)} %pack_kv.1), calls=%async_computation | async-start | bytes 2097152 | tf_op jit(solution)/shard_map/all_to_all | solution.py:355
  13.4 2.4 pack_qg.1
  15.8 24.4 %all-to-all-done = bf16[32,64,256]{2,1,0:T(8,128)(2,1)S(1)} async-done(((bf16[32,64,256]{2,1,0:T(8,128)(2,1)}), bf16[32,64,256]{2,1,0:T(8,128)(2,1)S(1)}, u32[]{:S(2)}, u32[]{:S(2)}) %all-to-all-start) | async-done | bytes 1048608 | tf_op jit(solution)/shard_map/all_to_all | solution.py:355
  40.2 5.0 %all-to-all-start.1 = ((bf16[32,64,256]{2,1,0:T(8,128)(2,1)}), bf16[32,64,256]{2,1,0:T(8,128)(2,1)S(1)}, u32[]{:S(2)}, u32[]{:S(2)}) async-start(bf16[32,64,256]{2,1,0:T(8,128)(2,1)} %pack_qg.1), calls=%async_computation.1 | async-start | bytes 2097152 | tf_op jit(solution)/shard_map/all_to_all | solution.py:355
  45.2 0.0 copy-done
  45.2 2.8 %levels.1 = (bf16[1024,256]{1,0:T(8,128)(2,1)}, bf16[512,256]{1,0:T(8,128)(2,1)}, bf16[128,256]{1,0:T(8,128)(2,1)}, bf16[512,256]{1,0:T(8,128)(2,1)}, bf16[512,256]{1,0:T(8,128)(2,1)}) custom-call(bf16[2048,256]{1,0:T(8,128)(2,1)} %bitcast.5), custom_call_target="tpu_custom_call" | custom-call | bytes 2097152 | tf_op jit(solution)/shard_map/levels/pallas_call | solution.py:334
  48.0 8.4 %collective-permute-start = (bf16[512,256]{1,0:T(8,128)(2,1)}, bf16[512,256]{1,0:T(8,128)(2,1)S(1)}, u32[]{:S(2)}, u32[]{:S(2)}) collective-permute-start(bf16[512,256]{1,0:T(8,128)(2,1)} %get-tuple-element.31), channel_id=1, source_target_pairs={{0,32},{32,64},{64,96},{96,128},{128,160},{160,192},{192,224},{224... | collective-permute-start | bytes 786440 | tf_op jit(solution)/shard_map/ppermute | solution.py:359
  56.4 1.3 collective-permute-start.1
  57.7 8.8 %collective-permute-start.3 = (bf16[128,256]{1,0:T(8,128)(2,1)}, bf16[128,256]{1,0:T(8,128)(2,1)S(1)}, u32[]{:S(2)}, u32[]{:S(2)}) collective-permute-start(bf16[128,256]{1,0:T(8,128)(2,1)} %get-tuple-element.33.l4_ref), channel_id=1, source_target_pairs={{0,96},{32,64},{64,32},{96,0},{1,97},{33,65},{65,33},{97,1},{2,98}... | collective-permute-start | bytes 196616 | tf_op jit(solution)/shard_map/ppermute | solution.py:362
  66.5 6.1 %collective-permute-start.2 = (bf16[128,256]{1,0:T(8,128)(2,1)}, bf16[128,256]{1,0:T(8,128)(2,1)S(1)}, u32[]{:S(2)}, u32[]{:S(2)}) collective-permute-start(bf16[128,256]{1,0:T(8,128)(2,1)} %get-tuple-element.33.l4_ref), channel_id=1, source_target_pairs={{0,64},{32,96},{64,0},{96,32},{1,65},{33,97},{65,1},{97,33},{2,66}... | collective-permute-start | bytes 196616 | tf_op jit(solution)/shard_map/ppermute | solution.py:362
  72.6 19.0 %collective-permute-done.3.z3_ref = bf16[128,256]{1,0:T(8,128)(2,1)S(1)} collective-permute-done((bf16[128,256]{1,0:T(8,128)(2,1)}, bf16[128,256]{1,0:T(8,128)(2,1)S(1)}, u32[]{:S(2)}, u32[]{:S(2)}) %collective-permute-start.3) | collective-permute-done | bytes 65568 | tf_op jit(solution)/shard_map/ppermute | solution.py:362
  91.7 7.2 %collective-permute-done.2.z2_ref = bf16[128,256]{1,0:T(8,128)(2,1)S(1)} collective-permute-done((bf16[128,256]{1,0:T(8,128)(2,1)}, bf16[128,256]{1,0:T(8,128)(2,1)S(1)}, u32[]{:S(2)}, u32[]{:S(2)}) %collective-permute-start.2) | collective-permute-done | bytes 65568 | tf_op jit(solution)/shard_map/ppermute | solution.py:362
  98.8 0.0 collective-permute-done.before_ref
  98.8 0.0 collective-permute-done.1.after_ref
  98.8 0.0 copy-start.7
  98.8 0.0 copy-done.11
  98.8 0.6 copy-done.12
  99.4 0.1 copy-done.6
  99.5 0.1 copy-done.7
  99.6 2.2 group.1
  101.9 3.2 %collective-permute-start.4 = (bf16[256,256]{1,0:T(8,128)(2,1)}, bf16[256,256]{1,0:T(8,128)(2,1)S(1)}, u32[]{:S(2)}, u32[]{:S(2)}) collective-permute-start(bf16[256,256]{1,0:T(8,128)(2,1)} %get-tuple-element.34), channel_id=1, source_target_pairs={{0,128},{128,0},{256,384},{384,256},{1,129},{129,1},{257,385},{385... | collective-permute-start | bytes 393224 | tf_op jit(solution)/shard_map/ppermute | solution.py:362
  105.1 3.8 %collective-permute-start.6 = (bf16[128,256]{1,0:T(8,128)(2,1)}, bf16[128,256]{1,0:T(8,128)(2,1)S(1)}, u32[]{:S(2)}, u32[]{:S(2)}) collective-permute-start(bf16[128,256]{1,0:T(8,128)(2,1)} %get-tuple-element.35), channel_id=1, source_target_pairs={{0,384},{128,256},{256,128},{384,0},{1,385},{129,257},{257,129},{3... | collective-permute-start | bytes 196616 | tf_op jit(solution)/shard_map/ppermute | solution.py:362
  108.9 2.0 collective-permute-start.5
  110.8 0.0 all-to-all-done.1
  110.9 0.0 copy-start.3
  110.9 0.6 collective-permute-done.6.y3_ref
  111.5 4.1 %collective-permute-done.5.y2_ref = bf16[128,256]{1,0:T(8,128)(2,1)S(1)} collective-permute-done((bf16[128,256]{1,0:T(8,128)(2,1)}, bf16[128,256]{1,0:T(8,128)(2,1)S(1)}, u32[]{:S(2)}, u32[]{:S(2)}) %collective-permute-start.5) | collective-permute-done | bytes 65568 | tf_op jit(solution)/shard_map/ppermute | solution.py:362
  115.6 0.0 collective-permute-done.4.y1_ref
  115.6 0.0 copy-done.3
  115.6 0.0 copy-done.17
  115.6 0.6 copy-done.19
  116.2 0.0 copy-done.15
  116.3 24.1 %attend.1 = (bf16[2048,256]{1,0:T(8,128)(2,1)}, f32[2048,256]{1,0:T(8,128)}, bf16[256,256]{1,0:T(8,128)(2,1)}, bf16[256,256]{1,0:T(8,128)(2,1)}, f32[256,256]{1,...) custom-call(s32[1]{0:T(128)} %bitcast.c_ref, ...), custom_call_target="tpu_custom_call" | custom-call | flops 4000000000 | bytes 7602184 | tf_op jit(solution)/shard_map/attend/pallas_call | solution.py:334
  140.4 16.3 %all-to-all-start.2 = ((bf16[32,64,256]{2,1,0:T(8,128)(2,1)}), bf16[32,64,256]{2,1,0:T(8,128)(2,1)S(1)}, u32[]{:S(2)}, u32[]{:S(2)}) async-start(bf16[32,64,256]{2,1,0:T(8,128)(2,1)} %bitcast.9), calls=%async_computation.2 | async-start | bytes 2097152 | tf_op jit(solution)/shard_map/all_to_all | solution.py:355
  156.7 2.2 collective-permute-start.7
  158.9 3.6 %collective-permute-start.8 = (bf16[128,256]{1,0:T(8,128)(2,1)S(1)}, bf16[128,256]{1,0:T(8,128)(2,1)S(1)}, u32[]{:S(2)}, u32[]{:S(2)}) collective-permute-start(bf16[128,256]{1,0:T(8,128)(2,1)S(1)} %copy-done.20), channel_id=1, source_target_pairs={{0,256},{128,384},{256,0},{384,128},{1,257},{129,385},{257,1},{385... | collective-permute-start | bytes 196616 | tf_op jit(solution)/shard_map/ppermute | solution.py:362
  162.5 0.0 copy-done.18
  162.5 3.8 %collective-permute-start.9 = (bf16[128,256]{1,0:T(8,128)(2,1)S(1)}, bf16[128,256]{1,0:T(8,128)(2,1)S(1)}, u32[]{:S(2)}, u32[]{:S(2)}) collective-permute-start(bf16[128,256]{1,0:T(8,128)(2,1)S(1)} %copy-done.18), channel_id=1, source_target_pairs={{0,384},{128,256},{256,128},{384,0},{1,385},{129,257},{257,129},{3... | collective-permute-start | bytes 196616 | tf_op jit(solution)/shard_map/ppermute | solution.py:362
  166.3 0.0 collective-permute-done.8.r2_ref
  166.3 0.0 copy-start.13
  166.3 2.7 %collective-permute-done.9.r3_ref = bf16[128,256]{1,0:T(8,128)(2,1)S(1)} collective-permute-done((bf16[128,256]{1,0:T(8,128)(2,1)S(1)}, bf16[128,256]{1,0:T(8,128)(2,1)S(1)}, u32[]{:S(2)}, u32[]{:S(2)}) %collective-permute-start.9) | collective-permute-done | bytes 65568 | tf_op jit(solution)/shard_map/ppermute | solution.py:362
  169.0 0.0 collective-permute-done.7.r1_ref
  169.0 0.6 copy-done.14
  169.6 0.1 copy-done.8
  169.7 2.2 fold.1
  171.9 6.1 %collective-permute-start.10 = (bf16[512,256]{1,0:T(8,128)(2,1)}, bf16[512,256]{1,0:T(8,128)(2,1)S(1)}, u32[]{:S(2)}, u32[]{:S(2)}) collective-permute-start(bf16[512,256]{1,0:T(8,128)(2,1)} %get-tuple-element.47), channel_id=1, source_target_pairs={{0,32},{32,64},{64,96},{96,128},{128,160},{160,192},{192,224},{224... | collective-permute-start | bytes 786440 | tf_op jit(solution)/shard_map/ppermute | solution.py:359
  178.0 1.3 collective-permute-start.11
  179.3 9.6 %collective-permute-start.12 = (bf16[128,256]{1,0:T(8,128)(2,1)}, bf16[128,256]{1,0:T(8,128)(2,1)S(1)}, u32[]{:S(2)}, u32[]{:S(2)}) collective-permute-start(bf16[128,256]{1,0:T(8,128)(2,1)} %get-tuple-element.49), channel_id=1, source_target_pairs={{0,64},{32,96},{64,0},{96,32},{1,65},{33,97},{65,1},{97,33},{2,66}... | collective-permute-start | bytes 196616 | tf_op jit(solution)/shard_map/ppermute | solution.py:362
  188.9 5.3 %collective-permute-start.13 = (bf16[128,256]{1,0:T(8,128)(2,1)}, bf16[128,256]{1,0:T(8,128)(2,1)S(1)}, u32[]{:S(2)}, u32[]{:S(2)}) collective-permute-start(bf16[128,256]{1,0:T(8,128)(2,1)} %get-tuple-element.50), channel_id=1, source_target_pairs={{0,96},{32,64},{64,32},{96,0},{1,97},{33,65},{65,33},{97,1},{2,98}... | collective-permute-start | bytes 196616 | tf_op jit(solution)/shard_map/ppermute | solution.py:362
  194.2 12.3 %collective-permute-done.12.z2_ref = bf16[128,256]{1,0:T(8,128)(2,1)S(1)} collective-permute-done((bf16[128,256]{1,0:T(8,128)(2,1)}, bf16[128,256]{1,0:T(8,128)(2,1)S(1)}, u32[]{:S(2)}, u32[]{:S(2)}) %collective-permute-start.12) | collective-permute-done | bytes 65568 | tf_op jit(solution)/shard_map/ppermute | solution.py:362
  206.5 0.0 collective-permute-done.13.z3_ref
  206.5 0.0 collective-permute-done.10.before_ref
  206.5 0.0 copy-start.4
  206.5 6.0 %collective-permute-done.11.after_ref = bf16[512,256]{1,0:T(8,128)(2,1)S(1)} collective-permute-done((bf16[512,256]{1,0:T(8,128)(2,1)}, bf16[512,256]{1,0:T(8,128)(2,1)S(1)}, u32[]{:S(2)}, u32[]{:S(2)}) %collective-permute-start.11) | collective-permute-done | bytes 262176 | tf_op jit(solution)/shard_map/ppermute | solution.py:359
  212.5 0.0 copy-done.10
  212.5 0.7 copy-done.5
  213.2 3.3 %combine.1 = bf16[2048,256]{1,0:T(8,128)(2,1)} custom-call(s32[1]{0:T(128)} %bitcast.c_ref, f32[2048,256]{1,0:T(8,128)} %get-tuple-element.39.d_ref, bf16[512,256]{1,0:T(8,128)(2,1)} %copy-done.4, bf16[512,256]{1,0:T(8,128)(2,1)} %copy-done.5, bf16[128,256]{1,0:T(8,128)(2,1)} %copy-done.9, bf16[128,256]{1,0:T(8,128)(2,1)} %copy-done.10, ...), custom_call_target="tpu_custom_call" | custom-call | bytes 5636104 | tf_op jit(solution)/shard_map/combine/pallas_call | solution.py:334
  216.5 0.0 all-to-all-done.2.x_ref
  216.5 11.9 %all-to-all-start.3 = ((bf16[32,64,256]{2,1,0:T(8,128)(2,1)}), bf16[32,64,256]{2,1,0:T(8,128)(2,1)S(1)}, u32[]{:S(2)}, u32[]{:S(2)}) async-start(bf16[32,64,256]{2,1,0:T(8,128)(2,1)} %bitcast.7), calls=%async_computation.3 | async-start | bytes 2097152 | tf_op jit(solution)/shard_map/all_to_all | solution.py:355
  228.4 2.5 unpack_ag.1
  230.9 24.2 %all-to-all-done.3.x_ref = bf16[32,64,256]{2,1,0:T(8,128)(2,1)S(1)} async-done(((bf16[32,64,256]{2,1,0:T(8,128)(2,1)}), bf16[32,64,256]{2,1,0:T(8,128)(2,1)S(1)}, u32[]{:S(2)}, u32[]{:S(2)}) %all-to-all-start.3) | async-done | bytes 1048608 | tf_op jit(solution)/shard_map/all_to_all | solution.py:355
  255.1 1.0 copy-done.2
  256.1 2.5 unpack_kv.1
  (23 shorter events, 0.0 us)
Async XLA Ops:
  3.0 37.2 %all-to-all-start = ((bf16[32,64,256]{2,1,0:T(8,128)(2,1)}), bf16[32,64,256]{2,1,0:T(8,128)(2,1)S(1)}, u32[]{:S(2)}, u32[]{:S(2)}) async-start(bf16[32,64,256]{2,1,0:T(8,128)(2,1)} %pack_kv.1), calls=%async_computation | async-start | bytes 2097152 | tf_op jit(solution)/shard_map/all_to_all | solution.py:355
  40.2 5.0 %copy-start = (bf16[32,64,256]{2,1,0:T(8,128)(2,1)}, bf16[32,64,256]{2,1,0:T(8,128)(2,1)S(1)}, u32[]{:S(2)}) copy-start(bf16[32,64,256]{2,1,0:T(8,128)(2,1)S(1)} %all-to-all-done) | copy-start | bytes 3145732
  40.2 70.6 %all-to-all-start.1 = ((bf16[32,64,256]{2,1,0:T(8,128)(2,1)}), bf16[32,64,256]{2,1,0:T(8,128)(2,1)S(1)}, u32[]{:S(2)}, u32[]{:S(2)}) async-start(bf16[32,64,256]{2,1,0:T(8,128)(2,1)} %pack_qg.1), calls=%async_computation.1 | async-start | bytes 2097152 | tf_op jit(solution)/shard_map/all_to_all | solution.py:355
  48.0 50.8 %collective-permute-start = (bf16[512,256]{1,0:T(8,128)(2,1)}, bf16[512,256]{1,0:T(8,128)(2,1)S(1)}, u32[]{:S(2)}, u32[]{:S(2)}) collective-permute-start(bf16[512,256]{1,0:T(8,128)(2,1)} %get-tuple-element.31), channel_id=1, source_target_pairs={{0,32},{32,64},{64,96},{96,128},{128,160},{160,192},{192,224},{224... | collective-permute-start | bytes 786440 | tf_op jit(solution)/shard_map/ppermute | solution.py:359
  56.4 42.4 %collective-permute-start.1 = (bf16[512,256]{1,0:T(8,128)(2,1)}, bf16[512,256]{1,0:T(8,128)(2,1)S(1)}, u32[]{:S(2)}, u32[]{:S(2)}) collective-permute-start(bf16[512,256]{1,0:T(8,128)(2,1)} %get-tuple-element.32), channel_id=1, source_target_pairs={{32,0},{64,32},{96,64},{128,96},{160,128},{192,160},{224,192},{256... | collective-permute-start | bytes 786440 | tf_op jit(solution)/shard_map/ppermute | solution.py:359
  57.7 34.0 %collective-permute-start.3 = (bf16[128,256]{1,0:T(8,128)(2,1)}, bf16[128,256]{1,0:T(8,128)(2,1)S(1)}, u32[]{:S(2)}, u32[]{:S(2)}) collective-permute-start(bf16[128,256]{1,0:T(8,128)(2,1)} %get-tuple-element.33.l4_ref), channel_id=1, source_target_pairs={{0,96},{32,64},{64,32},{96,0},{1,97},{33,65},{65,33},{97,1},{2,98}... | collective-permute-start | bytes 196616 | tf_op jit(solution)/shard_map/ppermute | solution.py:362
  66.5 32.3 %collective-permute-start.2 = (bf16[128,256]{1,0:T(8,128)(2,1)}, bf16[128,256]{1,0:T(8,128)(2,1)S(1)}, u32[]{:S(2)}, u32[]{:S(2)}) collective-permute-start(bf16[128,256]{1,0:T(8,128)(2,1)} %get-tuple-element.33.l4_ref), channel_id=1, source_target_pairs={{0,64},{32,96},{64,0},{96,32},{1,65},{33,97},{65,1},{97,33},{2,66}... | collective-permute-start | bytes 196616 | tf_op jit(solution)/shard_map/ppermute | solution.py:362
  91.7 7.2 %copy-start.11 = (bf16[128,256]{1,0:T(8,128)(2,1)}, bf16[128,256]{1,0:T(8,128)(2,1)S(1)}, u32[]{:S(2)}) copy-start(bf16[128,256]{1,0:T(8,128)(2,1)S(1)} %collective-permute-done.3.z3_ref) | copy-start | bytes 196612
  98.8 0.6 copy-start.12
  98.8 0.7 copy-start.6
  98.8 0.8 copy-start.7
  101.9 13.7 %collective-permute-start.4 = (bf16[256,256]{1,0:T(8,128)(2,1)}, bf16[256,256]{1,0:T(8,128)(2,1)S(1)}, u32[]{:S(2)}, u32[]{:S(2)}) collective-permute-start(bf16[256,256]{1,0:T(8,128)(2,1)} %get-tuple-element.34), channel_id=1, source_target_pairs={{0,128},{128,0},{256,384},{384,256},{1,129},{129,1},{257,385},{385... | collective-permute-start | bytes 393224 | tf_op jit(solution)/shard_map/ppermute | solution.py:362
  105.1 6.4 %collective-permute-start.6 = (bf16[128,256]{1,0:T(8,128)(2,1)}, bf16[128,256]{1,0:T(8,128)(2,1)S(1)}, u32[]{:S(2)}, u32[]{:S(2)}) collective-permute-start(bf16[128,256]{1,0:T(8,128)(2,1)} %get-tuple-element.35), channel_id=1, source_target_pairs={{0,384},{128,256},{256,128},{384,0},{1,385},{129,257},{257,129},{3... | collective-permute-start | bytes 196616 | tf_op jit(solution)/shard_map/ppermute | solution.py:362
  108.9 6.7 %collective-permute-start.5 = (bf16[128,256]{1,0:T(8,128)(2,1)}, bf16[128,256]{1,0:T(8,128)(2,1)S(1)}, u32[]{:S(2)}, u32[]{:S(2)}) collective-permute-start(bf16[128,256]{1,0:T(8,128)(2,1)} %get-tuple-element.35), channel_id=1, source_target_pairs={{0,256},{128,384},{256,0},{384,128},{1,257},{129,385},{257,1},{385... | collective-permute-start | bytes 196616 | tf_op jit(solution)/shard_map/ppermute | solution.py:362
  110.9 4.8 %copy-start.3 = (bf16[32,64,256]{2,1,0:T(8,128)(2,1)}, bf16[32,64,256]{2,1,0:T(8,128)(2,1)S(1)}, u32[]{:S(2)}) copy-start(bf16[32,64,256]{2,1,0:T(8,128)(2,1)S(1)} %all-to-all-done.1) | copy-start | bytes 3145732
  111.5 4.1 %copy-start.17 = (bf16[128,256]{1,0:T(8,128)(2,1)}, bf16[128,256]{1,0:T(8,128)(2,1)S(1)}, u32[]{:S(2)}) copy-start(bf16[128,256]{1,0:T(8,128)(2,1)S(1)} %collective-permute-done.6.y3_ref) | copy-start | bytes 196612
  115.6 0.6 copy-start.19
  115.6 0.7 copy-start.15
  140.4 16.3 %copy-start.16 = (bf16[256,256]{1,0:T(8,128)(2,1)S(1)}, bf16[256,256]{1,0:T(8,128)(2,1)}, u32[]{:S(2)}) copy-start(bf16[256,256]{1,0:T(8,128)(2,1)} %get-tuple-element.44) | copy-start | bytes 393220
  140.4 18.5 %copy-start.20 = (bf16[128,256]{1,0:T(8,128)(2,1)S(1)}, bf16[128,256]{1,0:T(8,128)(2,1)}, u32[]{:S(2)}) copy-start(bf16[128,256]{1,0:T(8,128)(2,1)} %get-tuple-element.45) | copy-start | bytes 196612
  140.4 22.1 %copy-start.18 = (bf16[128,256]{1,0:T(8,128)(2,1)S(1)}, bf16[128,256]{1,0:T(8,128)(2,1)}, u32[]{:S(2)}) copy-start(bf16[128,256]{1,0:T(8,128)(2,1)} %get-tuple-element.46) | copy-start | bytes 196612
  140.4 76.2 %all-to-all-start.2 = ((bf16[32,64,256]{2,1,0:T(8,128)(2,1)}), bf16[32,64,256]{2,1,0:T(8,128)(2,1)S(1)}, u32[]{:S(2)}, u32[]{:S(2)}) async-start(bf16[32,64,256]{2,1,0:T(8,128)(2,1)} %bitcast.9), calls=%async_computation.2 | async-start | bytes 2097152 | tf_op jit(solution)/shard_map/all_to_all | solution.py:355
  156.7 12.3 %collective-permute-start.7 = (bf16[256,256]{1,0:T(8,128)(2,1)S(1)}, bf16[256,256]{1,0:T(8,128)(2,1)S(1)}, u32[]{:S(2)}, u32[]{:S(2)}) collective-permute-start(bf16[256,256]{1,0:T(8,128)(2,1)S(1)} %copy-done.16), channel_id=1, source_target_pairs={{0,128},{128,0},{256,384},{384,256},{1,129},{129,1},{257,385},{385... | collective-permute-start | bytes 393224 | tf_op jit(solution)/shard_map/ppermute | solution.py:362
  158.9 7.5 %collective-permute-start.8 = (bf16[128,256]{1,0:T(8,128)(2,1)S(1)}, bf16[128,256]{1,0:T(8,128)(2,1)S(1)}, u32[]{:S(2)}, u32[]{:S(2)}) collective-permute-start(bf16[128,256]{1,0:T(8,128)(2,1)S(1)} %copy-done.20), channel_id=1, source_target_pairs={{0,256},{128,384},{256,0},{384,128},{1,257},{129,385},{257,1},{385... | collective-permute-start | bytes 196616 | tf_op jit(solution)/shard_map/ppermute | solution.py:362
  162.5 6.5 %collective-permute-start.9 = (bf16[128,256]{1,0:T(8,128)(2,1)S(1)}, bf16[128,256]{1,0:T(8,128)(2,1)S(1)}, u32[]{:S(2)}, u32[]{:S(2)}) collective-permute-start(bf16[128,256]{1,0:T(8,128)(2,1)S(1)} %copy-done.18), channel_id=1, source_target_pairs={{0,384},{128,256},{256,128},{384,0},{1,385},{129,257},{257,129},{3... | collective-permute-start | bytes 196616 | tf_op jit(solution)/shard_map/ppermute | solution.py:362
  166.3 2.7 %copy-start.13 = (bf16[128,256]{1,0:T(8,128)(2,1)}, bf16[128,256]{1,0:T(8,128)(2,1)S(1)}, u32[]{:S(2)}) copy-start(bf16[128,256]{1,0:T(8,128)(2,1)S(1)} %collective-permute-done.8.r2_ref) | copy-start | bytes 196612
  169.0 0.6 copy-start.14
  169.0 0.7 copy-start.8
  171.9 34.7 %collective-permute-start.10 = (bf16[512,256]{1,0:T(8,128)(2,1)}, bf16[512,256]{1,0:T(8,128)(2,1)S(1)}, u32[]{:S(2)}, u32[]{:S(2)}) collective-permute-start(bf16[512,256]{1,0:T(8,128)(2,1)} %get-tuple-element.47), channel_id=1, source_target_pairs={{0,32},{32,64},{64,96},{96,128},{128,160},{160,192},{192,224},{224... | collective-permute-start | bytes 786440 | tf_op jit(solution)/shard_map/ppermute | solution.py:359
  178.0 34.5 %collective-permute-start.11 = (bf16[512,256]{1,0:T(8,128)(2,1)}, bf16[512,256]{1,0:T(8,128)(2,1)S(1)}, u32[]{:S(2)}, u32[]{:S(2)}) collective-permute-start(bf16[512,256]{1,0:T(8,128)(2,1)} %get-tuple-element.48), channel_id=1, source_target_pairs={{32,0},{64,32},{96,64},{128,96},{160,128},{192,160},{224,192},{256... | collective-permute-start | bytes 786440 | tf_op jit(solution)/shard_map/ppermute | solution.py:359
  179.3 27.2 %collective-permute-start.12 = (bf16[128,256]{1,0:T(8,128)(2,1)}, bf16[128,256]{1,0:T(8,128)(2,1)S(1)}, u32[]{:S(2)}, u32[]{:S(2)}) collective-permute-start(bf16[128,256]{1,0:T(8,128)(2,1)} %get-tuple-element.49), channel_id=1, source_target_pairs={{0,64},{32,96},{64,0},{96,32},{1,65},{33,97},{65,1},{97,33},{2,66}... | collective-permute-start | bytes 196616 | tf_op jit(solution)/shard_map/ppermute | solution.py:362
  188.9 17.7 %collective-permute-start.13 = (bf16[128,256]{1,0:T(8,128)(2,1)}, bf16[128,256]{1,0:T(8,128)(2,1)S(1)}, u32[]{:S(2)}, u32[]{:S(2)}) collective-permute-start(bf16[128,256]{1,0:T(8,128)(2,1)} %get-tuple-element.50), channel_id=1, source_target_pairs={{0,96},{32,64},{64,32},{96,0},{1,97},{33,65},{65,33},{97,1},{2,98}... | collective-permute-start | bytes 196616 | tf_op jit(solution)/shard_map/ppermute | solution.py:362
  206.5 6.0 %copy-start.9 = (bf16[128,256]{1,0:T(8,128)(2,1)}, bf16[128,256]{1,0:T(8,128)(2,1)S(1)}, u32[]{:S(2)}) copy-start(bf16[128,256]{1,0:T(8,128)(2,1)S(1)} %collective-permute-done.12.z2_ref) | copy-start | bytes 196612
  206.5 6.0 %copy-start.10 = (bf16[128,256]{1,0:T(8,128)(2,1)}, bf16[128,256]{1,0:T(8,128)(2,1)S(1)}, u32[]{:S(2)}) copy-start(bf16[128,256]{1,0:T(8,128)(2,1)S(1)} %collective-permute-done.13.z3_ref) | copy-start | bytes 196612
  206.5 6.0 %copy-start.4 = (bf16[512,256]{1,0:T(8,128)(2,1)}, bf16[512,256]{1,0:T(8,128)(2,1)S(1)}, u32[]{:S(2)}) copy-start(bf16[512,256]{1,0:T(8,128)(2,1)S(1)} %collective-permute-done.10.before_ref) | copy-start | bytes 786436
  212.5 0.7 copy-start.5
  216.5 11.9 %copy-start.1 = (bf16[32,64,256]{2,1,0:T(8,128)(2,1)}, bf16[32,64,256]{2,1,0:T(8,128)(2,1)S(1)}, u32[]{:S(2)}) copy-start(bf16[32,64,256]{2,1,0:T(8,128)(2,1)S(1)} %all-to-all-done.2.x_ref) | copy-start | bytes 3145732
  216.5 38.5 %all-to-all-start.3 = ((bf16[32,64,256]{2,1,0:T(8,128)(2,1)}), bf16[32,64,256]{2,1,0:T(8,128)(2,1)S(1)}, u32[]{:S(2)}, u32[]{:S(2)}) async-start(bf16[32,64,256]{2,1,0:T(8,128)(2,1)} %bitcast.7), calls=%async_computation.3 | async-start | bytes 2097152 | tf_op jit(solution)/shard_map/all_to_all | solution.py:355
  255.1 1.0 copy-start.2

commit v2 on v1

--- a/solution.py
+++ b/solution.py
@@ -6,6 +6,7 @@
 from jax.experimental import pallas as pl
 from jax.experimental.pallas import tpu as pltpu
 from jax.sharding import Mesh, PartitionSpec as P
+
 
 HD = 128
 BLOCK = 256
@@ -87,56 +88,46 @@
         b_ref[:, h * HD : (h + 1) * HD] = x_ref[h, :, HD : 2 * HD]
 
 
-def levels_kernel(kv_ref, l1_ref, l2_ref, l4_ref, up_ref, down_ref):
+def levels_kernel(kv_ref, l1_ref, l2_ref, l3_ref, l4_ref):
     half = BLOCK // 2
     for b in range(8):
         l1_ref[b * half : (b + 1) * half, :] = coarsen(kv_ref[b * BLOCK : (b + 1) * BLOCK, :])
     for b in range(4):
         l2_ref[b * half : (b + 1) * half, :] = coarsen(l1_ref[b * BLOCK : (b + 1) * BLOCK, :])
     for b in range(2):
-        l3 = coarsen(l2_ref[b * BLOCK : (b + 1) * BLOCK, :])
-        up_ref[BLOCK + b * half : BLOCK + (b + 1) * half, :] = l3
-        down_ref[BLOCK + b * half : BLOCK + (b + 1) * half, :] = l3
-    l4_ref[...] = coarsen(up_ref[BLOCK : 2 * BLOCK, :])
-    up_ref[0:BLOCK, :] = kv_ref[ROWS - BLOCK : ROWS, :]
-    down_ref[0:BLOCK, :] = kv_ref[0:BLOCK, :]
-
-
-def group_kernel(c_ref, l4_ref, before_ref, after_ref, z2_ref, z3_ref, g5_ref, g6_ref):
-    even = c_ref[0] % 2 == 0
-    l3 = jnp.where(even, after_ref[BLOCK : 2 * BLOCK, :], before_ref[BLOCK : 2 * BLOCK, :])
-    g5_ref[0:64, :] = coarsen(l4_ref[...])
-    g5_ref[64:128, :] = coarsen(coarsen(l3))
-    g5_ref[128:192, :] = coarsen(z2_ref[...])
-    g5_ref[192:256, :] = coarsen(z3_ref[...])
-    g6_ref[...] = coarsen(g5_ref[...])
+        l3_ref[b * half : (b + 1) * half, :] = coarsen(l2_ref[b * BLOCK : (b + 1) * BLOCK, :])
+    l4_ref[...] = coarsen(l3_ref[...])
+
+
+def group_kernel(l4_ref, z1_ref, z2_ref, z3_ref, o_ref):
+    parts = (l4_ref[...], coarsen(z1_ref[...]), z2_ref[...], z3_ref[...])
+    for k, part in enumerate(parts):
+        o_ref[k * 64 : (k + 1) * 64, :] = coarsen(part)
 
 
 def main_kernel(
-    c_ref, kv_ref, qg_ref, l1_ref, l2_ref, before_ref, after_ref, z2_ref, z3_ref, y1_ref, y2_ref, y3_ref,
-    ag_ref, d_ref, ups_ref, downs_ref, g3_ref, g4_ref, t1_ref, t2_ref, t3_ref,
+    c_ref, kv_ref, qg_ref, l1_ref, l2_ref, before_ref, after_ref, z1_ref, z2_ref, z3_ref, y_ref,
+    ag_ref, d_ref, up_ref, down_ref, w1_ref, w2_ref, t1_ref, t2_ref, t3_ref,
     kx, gkx, qc, sib, gs, w_s, u_s, s_s, acc_s, e_s, po_s, pd_s, gq_s, gq0, tmp,
 ):
     c = c_ref[0]
     half = BLOCK // 2
-    even = c % 2 == 0
-
-    kx[0:BLOCK, :] = before_ref[0:BLOCK, :]
+
+    kx[0:BLOCK, :] = before_ref[...]
     kx[BLOCK : BLOCK + ROWS, :] = kv_ref[...]
-    kx[BLOCK + ROWS :, :] = after_ref[0:BLOCK, :]
+    kx[BLOCK + ROWS :, :] = after_ref[...]
     gkx[...] = jnp.zeros_like(gkx)
     for b in range(4):
         sib[SIB[1] + b * BLOCK : SIB[1] + (b + 1) * BLOCK, :] = l1_ref[(b ^ 1) * BLOCK : ((b ^ 1) + 1) * BLOCK, :]
     for b in range(2):
         sib[SIB[2] + b * BLOCK : SIB[2] + (b + 1) * BLOCK, :] = l2_ref[(b ^ 1) * BLOCK : ((b ^ 1) + 1) * BLOCK, :]
-    sib[SIB[3] : SIB[3] + BLOCK, :] = jnp.where(
-        even, after_ref[BLOCK : 2 * BLOCK, :], before_ref[BLOCK : 2 * BLOCK, :]
-    )
+    sib[SIB[3] : SIB[3] + BLOCK, :] = z1_ref[...]
     sib[SIB[4] : SIB[4] + half, :] = z2_ref[...]
     sib[SIB[4] + half : SIB[4] + BLOCK, :] = z3_ref[...]
-    sib[SIB[5] : SIB[5] + BLOCK, :] = y1_ref[...]
-    sib[SIB[6] : SIB[6] + half, :] = y2_ref[...]
-    sib[SIB[6] + half : SIB[6] + BLOCK, :] = y3_ref[...]
+    y = c // 4
+    sib[SIB[5] : SIB[5] + BLOCK, :] = y_ref[y ^ 1]
+    sib[SIB[6] : SIB[6] + half, :] = coarsen(y_ref[y ^ 2])
+    sib[SIB[6] + half : SIB[6] + BLOCK, :] = coarsen(y_ref[y ^ 3])
 
     for b in range(8):
         qc[b * half : (b + 1) * half, :] = coarsen(qg_ref[b * BLOCK : (b + 1) * BLOCK, 0:HD])
@@ -275,42 +266,33 @@
         return carry
 
     lax.fori_loop(0, CHUNK_BLOCKS, finish, 0)
-    downs_ref[...] = gkx[0:BLOCK, :].astype(bf16)
-    ups_ref[...] = gkx[BLOCK + ROWS :, :].astype(bf16)
-    g3_ref[...] = gs[SIB[3] : SIB[3] + BLOCK, :]
-    g4_ref[...] = gs[SIB[4] : SIB[4] + BLOCK, :]
+    down_ref[...] = gkx[0:BLOCK, :].astype(bf16)
+    up_ref[...] = gkx[BLOCK + ROWS :, :].astype(bf16)
+    w1_ref[...] = gs[SIB[3] : SIB[3] + BLOCK, :]
+    w2_ref[...] = gs[SIB[4] : SIB[4] + BLOCK, :]
     t1_ref[...] = gs[SIB[5] : SIB[5] + BLOCK, :].astype(bf16)
     t2_ref[...] = gs[SIB[6] : SIB[6] + half, :].astype(bf16)
     t3_ref[...] = gs[SIB[6] + half : SIB[6] + BLOCK, :].astype(bf16)
 
 
-def fold_kernel(
-    ups_ref, downs_ref, g3_ref, g4_ref, r1_ref, r2_ref, r3_ref, up_ref, down_ref, z2_ref, z3_ref, own_ref, tmp
-):
+def fold_kernel(r1_ref, r2_ref, r3_ref, w1_ref, w2_ref, own_ref, z1_ref, z2_ref, z3_ref, tmp):
     def rep2(x):
         return rep_pair(x * 0.5, tmp.at[0], tmp.at[1])
 
-    g6 = r2_ref[...].astype(f32) + r3_ref[...].astype(f32)
-    g5 = r1_ref[...].astype(f32) + rep2(g6)
+    half = BLOCK // 2
+    g5 = r1_ref[...].astype(f32) + rep2(r2_ref[...].astype(f32) + r3_ref[...].astype(f32))
     own_ref[...] = g5[0:64, :]
-    l3 = (g3_ref[...] + rep2(rep2(g5[64:128, :]))).astype(bf16)
-    up_ref[0:BLOCK, :] = ups_ref[...]
-    up_ref[BLOCK : 2 * BLOCK, :] = l3
-    down_ref[0:BLOCK, :] = downs_ref[...]
-    down_ref[BLOCK : 2 * BLOCK, :] = l3
-    z2_ref[...] = (g4_ref[0:128, :] + rep2(g5[128:192, :])).astype(bf16)
-    z3_ref[...] = (g4_ref[128:256, :] + rep2(g5[192:256, :])).astype(bf16)
-
-
-def combine_kernel(c_ref, d_ref, before_ref, after_ref, z2_ref, z3_ref, own_ref, o_ref, tmp, a_s, b_s):
-    even = c_ref[0] % 2 == 0
-
+    z1_ref[...] = (w1_ref[...] + rep2(rep2(g5[64:128, :]))).astype(bf16)
+    z2_ref[...] = (w2_ref[0:half, :] + rep2(g5[128:192, :])).astype(bf16)
+    z3_ref[...] = (w2_ref[half:BLOCK, :] + rep2(g5[192:256, :])).astype(bf16)
+
+
+def combine_kernel(d_ref, before_ref, after_ref, z1_ref, z2_ref, z3_ref, own_ref, o_ref, tmp, a_s, b_s):
     def rep2(x):
         return rep_pair(x * 0.5, tmp.at[0], tmp.at[1])
 
-    l3 = jnp.where(even, after_ref[BLOCK : 2 * BLOCK, :], before_ref[BLOCK : 2 * BLOCK, :])
     g4 = z2_ref[...].astype(f32) + z3_ref[...].astype(f32) + rep2(own_ref[...])
-    g3 = l3.astype(f32) + rep2(g4)
+    g3 = z1_ref[...].astype(f32) + rep2(g4)
     half = BLOCK // 2
     for b in range(2):
         a_s[b * BLOCK : (b + 1) * BLOCK, :] = rep2(g3[b * half : (b + 1) * half, :])
@@ -319,9 +301,9 @@
     for b in range(8):
         total = d_ref[b * BLOCK : (b + 1) * BLOCK, :] + rep2(b_s[b * half : (b + 1) * half, :])
         if b == 0:
-            total = total + before_ref[0:BLOCK, :].astype(f32)
+            total = total + before_ref[...].astype(f32)
         if b == 7:
-            total = total + after_ref[0:BLOCK, :].astype(f32)
+            total = total + after_ref[...].astype(f32)
         o_ref[b * BLOCK : (b + 1) * BLOCK, :] = total.astype(bf16)
 
 
@@ -329,11 +311,10 @@
     return jax.ShapeDtypeStruct(dims, dtype)
 
 
-def call(kernel, name, out_shape, scalars, args, scratch=(), flops=0):
+def call(kernel, out_shape, scalars, args, scratch=(), flops=0):
     nbytes = sum(a.size * a.dtype.itemsize for a in args)
     return pl.pallas_call(
         kernel,
-        name=name,
         out_shape=out_shape,
         in_specs=[SMEM] * scalars + [VMEM] * (len(args) - scalars),
         out_specs=jax.tree.map(lambda _: VMEM, out_shape),
@@ -345,11 +326,11 @@
 def per_device(queries, key_rows, value_rows, cotangent):
     own_rows, width = queries.shape
     heads = width // HD
-    peers = heads
     chunk = (lax.axis_index("y") * lax.axis_size("zh") + lax.axis_index("zh")).astype(jnp.int32).reshape(1)
-
-    def pack(a, b, name):
-        return call(pack_kernel, name, shape(bf16, heads, own_rows, 2 * HD), 0, (a, b))
+    wide = 2 * HD
+
+    def pack(a, b):
+        return call(pack_kernel, shape(bf16, heads, own_rows, wide), 0, (a, b))
 
     def swap(x):
         return lax.all_to_all(x, ("zl", "h"), split_axis=0, concat_axis=0, tiled=True)
@@ -361,56 +342,42 @@
     def flip(x, axis, bits):
         return lax.ppermute(x, axis, [(i, i ^ bits) for i in range(4)])
 
-    kv = swap(pack(key_rows, value_rows, "pack_kv")).reshape(ROWS, 2 * HD)
-    l1, l2, l4, up, down = call(
+    kv = swap(pack(key_rows, value_rows)).reshape(ROWS, wide)
+    l1, l2, l3, l4 = call(
         levels_kernel,
-        "levels",
-        (
-            shape(bf16, 1024, 2 * HD),
-            shape(bf16, 512, 2 * HD),
-            shape(bf16, 128, 2 * HD),
-            shape(bf16, 2 * BLOCK, 2 * HD),
-            shape(bf16, 2 * BLOCK, 2 * HD),
-        ),
+        (shape(bf16, 1024, wide), shape(bf16, 512, wide), shape(bf16, 256, wide), shape(bf16, 128, wide)),
         0,
         (kv,),
     )
-    before, after = shift(up, 1), shift(down, -1)
-    z2, z3 = flip(l4, "zh", 2), flip(l4, "zh", 3)
-    packed = pack(queries, cotangent, "pack_qg")
-    qg = swap(packed).reshape(ROWS, 2 * HD)
-    g5, g6 = call(
-        group_kernel,
-        "group",
-        (shape(bf16, BLOCK, 2 * HD), shape(bf16, 128, 2 * HD)),
-        1,
-        (chunk, l4, before, after, z2, z3),
-    )
-    y1, y2, y3 = flip(g5, "y", 1), flip(g6, "y", 2), flip(g6, "y", 3)
+    z1, z2, z3 = flip(l3, "zh", 1), flip(l4, "zh", 2), flip(l4, "zh", 3)
+    before = shift(kv[ROWS - BLOCK :], 1)
+    after = shift(kv[:BLOCK], -1)
+    qg = swap(pack(queries, cotangent)).reshape(ROWS, wide)
+    group = call(group_kernel, shape(bf16, BLOCK, wide), 0, (l4, z1, z2, z3))
+    far = lax.all_gather(group, "y")
     coarse = pltpu.VMEM((COARSE_ROWS, HD), f32)
-    ag, d, ups, downs, g3, g4, t1, t2, t3 = call(
+    ag, d, up, down, w1, w2, t1, t2, t3 = call(
         main_kernel,
-        "attend",
         (
-            shape(bf16, ROWS, 2 * HD),
-            shape(f32, ROWS, 2 * HD),
-            shape(bf16, BLOCK, 2 * HD),
-            shape(bf16, BLOCK, 2 * HD),
-            shape(f32, BLOCK, 2 * HD),
-            shape(f32, BLOCK, 2 * HD),
-            shape(bf16, BLOCK, 2 * HD),
-            shape(bf16, 128, 2 * HD),
-            shape(bf16, 128, 2 * HD),
+            shape(bf16, ROWS, wide),
+            shape(f32, ROWS, wide),
+            shape(bf16, BLOCK, wide),
+            shape(bf16, BLOCK, wide),
+            shape(f32, BLOCK, wide),
+            shape(f32, BLOCK, wide),
+            shape(bf16, BLOCK, wide),
+            shape(bf16, 128, wide),
+            shape(bf16, 128, wide),
         ),
         1,
-        (chunk, kv, qg, l1, l2, before, after, z2, z3, y1, y2, y3),
+        (chunk, kv, qg, l1, l2, before, after, z1, z2, z3, far),
         scratch=(
-            pltpu.VMEM((ROWS + 2 * BLOCK, 2 * HD), bf16),
-            pltpu.VMEM((ROWS + 2 * BLOCK, 2 * HD), f32),
+            pltpu.VMEM((ROWS + 2 * BLOCK, wide), bf16),
+            pltpu.VMEM((ROWS + 2 * BLOCK, wide), f32),
             pltpu.VMEM((COARSE_ROWS, HD), bf16),
-            pltpu.VMEM((SIB_ROWS, 2 * HD), bf16),
-            pltpu.VMEM((SIB_ROWS, 2 * HD), f32),
-            pltpu.VMEM((COARSE_ROWS, 2 * HD), f32),
+            pltpu.VMEM((SIB_ROWS, wide), bf16),
+            pltpu.VMEM((SIB_ROWS, wide), f32),
+            pltpu.VMEM((COARSE_ROWS, wide), f32),
             coarse,
             coarse,
             coarse,
@@ -423,50 +390,35 @@
         ),
         flops=4_000_000_000,
     )
-    out_ag = swap(ag.reshape(peers, own_rows, 2 * HD))
+    out_ag = swap(ag.reshape(heads, own_rows, wide))
     r1, r2, r3 = flip(t1, "y", 1), flip(t2, "y", 2), flip(t3, "y", 3)
-    up, down, z2, z3, own5 = call(
+    before = shift(up, 1)
+    after = shift(down, -1)
+    two = pltpu.VMEM((2, BLOCK, HD), f32)
+    own5, w1, w2, w3 = call(
         fold_kernel,
-        "fold",
-        (
-            shape(bf16, 2 * BLOCK, 2 * HD),
-            shape(bf16, 2 * BLOCK, 2 * HD),
-            shape(bf16, 128, 2 * HD),
-            shape(bf16, 128, 2 * HD),
-            shape(f32, 64, 2 * HD),
-        ),
+        (shape(f32, 64, wide), shape(bf16, BLOCK, wide), shape(bf16, 128, wide), shape(bf16, 128, wide)),
         0,
-        (ups, downs, g3, g4, r1, r2, r3),
-        scratch=(pltpu.VMEM((2, BLOCK, HD), f32),),
+        (r1, r2, r3, w1, w2),
+        scratch=(two,),
     )
-    before, after = shift(up, 1), shift(down, -1)
-    z2, z3 = flip(z2, "zh", 2), flip(z3, "zh", 3)
+    z1, z2, z3 = flip(w1, "zh", 1), flip(w2, "zh", 2), flip(w3, "zh", 3)
     gkv = call(
         combine_kernel,
-        "combine",
-        shape(bf16, ROWS, 2 * HD),
-        1,
-        (chunk, d, before, after, z2, z3, own5),
-        scratch=(
-            pltpu.VMEM((2, BLOCK, HD), f32),
-            pltpu.VMEM((512, 2 * HD), f32),
-            pltpu.VMEM((1024, 2 * HD), f32),
-        ),
+        shape(bf16, ROWS, wide),
+        0,
+        (d, before, after, z1, z2, z3, own5),
+        scratch=(two, pltpu.VMEM((512, wide), f32), pltpu.VMEM((1024, wide), f32)),
     )
-    out_kv = swap(gkv.reshape(peers, own_rows, 2 * HD))
+    out_kv = swap(gkv.reshape(heads, own_rows, wide))
     pair = (shape(bf16, own_rows, width), shape(bf16, own_rows, width))
-    attended, grad_query = call(unpack_kernel, "unpack_ag", pair, 0, (out_ag,))
-    grad_key, grad_value = call(unpack_kernel, "unpack_kv", pair, 0, (out_kv,))
+    attended, grad_query = call(unpack_kernel, pair, 0, (out_ag,))
+    grad_key, grad_value = call(unpack_kernel, pair, 0, (out_kv,))
     return attended, grad_query, grad_key, grad_value
 
 
 def solution(mesh):
     grid = Mesh(mesh.devices.reshape(4, 4, 4, 8), ("y", "zh", "zl", "h"))
     spec = P(("y", "zh", "zl", "h"), None)
-    return jax.shard_map(
-        per_device,
-        mesh=grid,
-        in_specs=(spec,) * 4,
-        out_specs=(spec,) * 4,
-        check_vma=False,
-    )
+
+    return jax.shard_map(per_device, mesh=grid, in_specs=(spec,) * 4, out_specs=(spec,) * 4, check_vma=False)

time: 260 us -> 246 us (0.946)
  waiting for transfers between devices: 100 us -> 72.9 us
  blocking collectives: 0 us -> 13.9 us
    ppermute x10 -> x9, waiting for transfers between devices: 45.9 us -> 24.4 us  [flip(): return lax.ppermute(x, axis, [(i, i ^ bits) for i in range(4)])]
    all_gather x0 -> x1, blocking collectives: none -> 13.9 us  [per_device(): far = lax.all_gather(group, 'y')]
    ppermute x4, waiting for transfers between devices: 5.99 us -> 0.01 us  [shift(): return lax.ppermute(x, ('y', 'zh'), pairs)]
    all_to_all x4, starting transfers between devices: 43.6 us -> 47.3 us  [swap(): lax.all_to_all(x, ('zl', 'h'), split_axis=0, concat_axis=0, tiled=True)]
    ppermute x10 -> x9, starting transfers between devices: 48.3 us -> 44.6 us  [flip(): return lax.ppermute(x, axis, [(i, i ^ bits) for i in range(4)])]
  transfers between devices with their start and end apart: 18 -> 17, of which waited for: 9 -> 7; matrix products, arithmetic and copies ran while one was open for 0% -> 0% of each run, Pallas kernels for 6% -> 6%
where the time goes in v2:
time: 246 us; the launch traced here: 244 us
  starting transfers between devices  108 us (44%)
  waiting for transfers between devices  72.9 us (30%)
  Pallas kernels  43.9 us (18%)
  blocking collectives  13.9 us (6%)
  local copies, waits for them, and re-layouts  5.07 us (2%)
    all_to_all x4, waiting for transfers between devices, swap(): lax.all_to_all(x, ('zl', 'h'), split_axis=0, concat_axis=0, tiled=True)  48.6 us
    all_to_all x4, starting transfers between devices, swap(): lax.all_to_all(x, ('zl', 'h'), split_axis=0, concat_axis=0, tiled=True)  47.3 us
    ppermute x9, starting transfers between devices, flip(): return lax.ppermute(x, axis, [(i, i ^ bits) for i in range(4)])  44.6 us
    pallas_call x9, Pallas kernels, call(): pl.pallas_call(kernel, out_shape=out_shape, in_specs=[SMEM] * scalars + [...  43.9 us
    ppermute x9, waiting for transfers between devices, flip(): return lax.ppermute(x, axis, [(i, i ^ bits) for i in range(4)])  24.4 us
    ppermute x4, starting transfers between devices, shift(): return lax.ppermute(x, ('y', 'zh'), pairs)  15.7 us
    all_gather x1, blocking collectives, per_device(): far = lax.all_gather(group, 'y')  13.9 us
  transfers between devices with their start and end apart: 17, of which 7 were waited for; matrix products, arithmetic and copies ran while one was open for 0% of the time, Pallas kernels for 6%

profile of v2, /device:TPU:1, one launch (start us, length us, event | category | flops | bytes accessed | tf_op | source)
XLA Modules:
  0.0 244.4 jit_solution(13006641137557939465)
XLA Ops:
  0.6 2.4 shard_map.75
  3.0 10.4 %all-to-all-start = ((bf16[32,64,256]{2,1,0:T(8,128)(2,1)}), bf16[32,64,256]{2,1,0:T(8,128)(2,1)S(1)}, u32[]{:S(2)}, u32[]{:S(2)}) async-start(bf16[32,64,256]{2,1,0:T(8,128)(2,1)} %shard_map.75), calls=%async_computation | async-start | bytes 2097152 | tf_op jit(solution)/shard_map/all_to_all | solution.py:336
  13.4 2.4 shard_map.76
  15.8 24.4 %all-to-all-done = bf16[32,64,256]{2,1,0:T(8,128)(2,1)S(1)} async-done(((bf16[32,64,256]{2,1,0:T(8,128)(2,1)}), bf16[32,64,256]{2,1,0:T(8,128)(2,1)S(1)}, u32[]{:S(2)}, u32[]{:S(2)}) %all-to-all-start) | async-done | bytes 1048608 | tf_op jit(solution)/shard_map/all_to_all | solution.py:336
  40.2 5.0 %all-to-all-start.1 = ((bf16[32,64,256]{2,1,0:T(8,128)(2,1)}), bf16[32,64,256]{2,1,0:T(8,128)(2,1)S(1)}, u32[]{:S(2)}, u32[]{:S(2)}) async-start(bf16[32,64,256]{2,1,0:T(8,128)(2,1)} %shard_map.76), calls=%async_computation.1 | async-start | bytes 2097152 | tf_op jit(solution)/shard_map/all_to_all | solution.py:336
  45.2 0.0 copy-done
  45.2 2.6 %shard_map.77 = (bf16[1024,256]{1,0:T(8,128)(2,1)}, bf16[512,256]{1,0:T(8,128)(2,1)}, bf16[256,256]{1,0:T(8,128)(2,1)}, bf16[128,256]{1,0:T(8,128)(2,1)}) custom-call(bf16[2048,256]{1,0:T(8,128)(2,1)} %bitcast.8), custom_call_target="tpu_custom_call" | custom-call | bytes 2097152 | tf_op jit(solution)/shard_map/pallas_call | solution.py:316
  47.9 9.3 %collective-permute-start.4 = (bf16[128,256]{1,0:T(8,128)(2,1)}, bf16[128,256]{1,0:T(8,128)(2,1)S(1)}, u32[]{:S(2)}, u32[]{:S(2)}) collective-permute-start(bf16[128,256]{1,0:T(8,128)(2,1)} %get-tuple-element.28.l4_ref), channel_id=1, source_target_pairs={{0,96},{32,64},{64,32},{96,0},{1,97},{33,65},{65,33},{97,1},{2,98}... | collective-permute-start | bytes 196616 | tf_op jit(solution)/shard_map/ppermute | solution.py:343
  57.2 6.1 %collective-permute-start.3 = (bf16[128,256]{1,0:T(8,128)(2,1)}, bf16[128,256]{1,0:T(8,128)(2,1)S(1)}, u32[]{:S(2)}, u32[]{:S(2)}) collective-permute-start(bf16[128,256]{1,0:T(8,128)(2,1)} %get-tuple-element.28.l4_ref), channel_id=1, source_target_pairs={{0,64},{32,96},{64,0},{96,32},{1,65},{33,97},{65,1},{97,33},{2,66}... | collective-permute-start | bytes 196616 | tf_op jit(solution)/shard_map/ppermute | solution.py:343
  63.2 2.9 %collective-permute-start.2 = (bf16[256,256]{1,0:T(8,128)(2,1)}, bf16[256,256]{1,0:T(8,128)(2,1)S(1)}, u32[]{:S(2)}, u32[]{:S(2)}) collective-permute-start(bf16[256,256]{1,0:T(8,128)(2,1)} %get-tuple-element.27), channel_id=1, source_target_pairs={{0,32},{32,0},{64,96},{96,64},{1,33},{33,1},{65,97},{97,65},{2,34}... | collective-permute-start | bytes 393224 | tf_op jit(solution)/shard_map/ppermute | solution.py:343
  66.1 1.0 fusion
  67.1 6.3 %collective-permute-start = (bf16[256,256]{1,0:T(8,128)(2,1)S(1)}, bf16[256,256]{1,0:T(8,128)(2,1)S(1)}, u32[]{:S(2)}, u32[]{:S(2)}) collective-permute-start(bf16[256,256]{1,0:T(8,128)(2,1)S(1)} %bitcast.15), channel_id=1, source_target_pairs={{0,32},{32,64},{64,96},{96,128},{128,160},{160,192},{192,224},{224... | collective-permute-start | bytes 393224 | tf_op jit(solution)/shard_map/ppermute | solution.py:340
  73.4 1.3 collective-permute-start.1
  74.7 0.1 collective-permute-done.4.z3_ref
  74.8 6.0 %collective-permute-done.3.z2_ref = bf16[128,256]{1,0:T(8,128)(2,1)S(1)} collective-permute-done((bf16[128,256]{1,0:T(8,128)(2,1)}, bf16[128,256]{1,0:T(8,128)(2,1)S(1)}, u32[]{:S(2)}, u32[]{:S(2)}) %collective-permute-start.3) | collective-permute-done | bytes 65568 | tf_op jit(solution)/shard_map/ppermute | solution.py:343
  80.8 1.9 collective-permute-done.2.z1_ref
  82.7 0.6 copy-done.6
  83.4 2.0 shard_map.78
  85.3 13.9 %all-gather = bf16[1024,256]{1,0:T(8,128)(2,1)} all-gather(bf16[256,256]{1,0:T(8,128)(2,1)} %shard_map.78), channel_id=2, replica_groups=mesh['y'=4,'zh'=4,'zl'=4,'h'=8] {'y'}, dimensions={0}, use_global_device_ids=true | all-gather | bytes 655360 | tf_op jit(solution)/shard_map/all_gather | solution.py:357
  99.2 0.0 all-to-all-done.1
  99.3 0.0 collective-permute-done.before_ref
  99.3 0.0 collective-permute-done.1.after_ref
  99.3 1.0 copy-done.3
  100.2 0.1 copy-done.17
  100.3 0.1 copy-done.19
  100.4 24.2 %shard_map.79 = (bf16[2048,256]{1,0:T(8,128)(2,1)}, f32[2048,256]{1,0:T(8,128)}, bf16[256,256]{1,0:T(8,128)(2,1)}, bf16[256,256]{1,0:T(8,128)(2,1)}, f32[256,256...) custom-call(s32[1]{0:T(128)} %bitcast.c_ref, ...), custom_call_target="tpu_custom_call" | custom-call | flops 4000000000 | bytes 7864328 | tf_op jit(solution)/shard_map/pallas_call | solution.py:316
  124.6 24.6 %all-to-all-start.2 = ((bf16[32,64,256]{2,1,0:T(8,128)(2,1)}), bf16[32,64,256]{2,1,0:T(8,128)(2,1)S(1)}, u32[]{:S(2)}, u32[]{:S(2)}) async-start(bf16[32,64,256]{2,1,0:T(8,128)(2,1)} %bitcast.11), calls=%async_computation.2 | async-start | bytes 2097152 | tf_op jit(solution)/shard_map/all_to_all | solution.py:336
  149.2 2.0 collective-permute-start.7
  151.2 0.0 copy-done.21
  151.2 4.3 %collective-permute-start.8 = (bf16[128,256]{1,0:T(8,128)(2,1)S(1)}, bf16[128,256]{1,0:T(8,128)(2,1)S(1)}, u32[]{:S(2)}, u32[]{:S(2)}) collective-permute-start(bf16[128,256]{1,0:T(8,128)(2,1)S(1)} %copy-done.21), channel_id=1, source_target_pairs={{0,256},{128,384},{256,0},{384,128},{1,257},{129,385},{257,1},{385... | collective-permute-start | bytes 196616 | tf_op jit(solution)/shard_map/ppermute | solution.py:343
  155.5 3.3 %collective-permute-start.9 = (bf16[128,256]{1,0:T(8,128)(2,1)S(1)}, bf16[128,256]{1,0:T(8,128)(2,1)S(1)}, u32[]{:S(2)}, u32[]{:S(2)}) collective-permute-start(bf16[128,256]{1,0:T(8,128)(2,1)S(1)} %copy-done.20), channel_id=1, source_target_pairs={{0,384},{128,256},{256,128},{384,0},{1,385},{129,257},{257,129},{3... | collective-permute-start | bytes 196616 | tf_op jit(solution)/shard_map/ppermute | solution.py:343
  158.9 0.0 copy-done.16
  158.9 6.8 %collective-permute-start.5 = (bf16[256,256]{1,0:T(8,128)(2,1)S(1)}, bf16[256,256]{1,0:T(8,128)(2,1)S(1)}, u32[]{:S(2)}, u32[]{:S(2)}) collective-permute-start(bf16[256,256]{1,0:T(8,128)(2,1)S(1)} %copy-done.16), channel_id=1, source_target_pairs={{0,32},{32,64},{64,96},{96,128},{128,160},{160,192},{192,224},{224... | collective-permute-start | bytes 393224 | tf_op jit(solution)/shard_map/ppermute | solution.py:340
  165.7 1.3 collective-permute-start.6
  167.0 0.0 collective-permute-done.8.r2_ref
  167.0 0.0 copy-start.13
  167.0 0.0 collective-permute-done.9.r3_ref
  167.0 0.0 collective-permute-done.7.r1_ref
  167.0 0.0 copy-start.8
  167.0 0.6 copy-done.13
  167.6 0.0 copy-done.14
  167.6 0.0 copy-done.8
  167.7 2.0 shard_map.81
  169.7 7.9 %collective-permute-start.10 = (bf16[256,256]{1,0:T(8,128)(2,1)}, bf16[256,256]{1,0:T(8,128)(2,1)S(1)}, u32[]{:S(2)}, u32[]{:S(2)}) collective-permute-start(bf16[256,256]{1,0:T(8,128)(2,1)} %get-tuple-element.40), channel_id=1, source_target_pairs={{0,32},{32,0},{64,96},{96,64},{1,33},{33,1},{65,97},{97,65},{2,34}... | collective-permute-start | bytes 393224 | tf_op jit(solution)/shard_map/ppermute | solution.py:343
  177.6 4.3 %collective-permute-start.11 = (bf16[128,256]{1,0:T(8,128)(2,1)}, bf16[128,256]{1,0:T(8,128)(2,1)S(1)}, u32[]{:S(2)}, u32[]{:S(2)}) collective-permute-start(bf16[128,256]{1,0:T(8,128)(2,1)} %get-tuple-element.41), channel_id=1, source_target_pairs={{0,64},{32,96},{64,0},{96,32},{1,65},{33,97},{65,1},{97,33},{2,66}... | collective-permute-start | bytes 196616 | tf_op jit(solution)/shard_map/ppermute | solution.py:343
  181.9 4.7 %collective-permute-start.12 = (bf16[128,256]{1,0:T(8,128)(2,1)}, bf16[128,256]{1,0:T(8,128)(2,1)S(1)}, u32[]{:S(2)}, u32[]{:S(2)}) collective-permute-start(bf16[128,256]{1,0:T(8,128)(2,1)} %get-tuple-element.42), channel_id=1, source_target_pairs={{0,96},{32,64},{64,32},{96,0},{1,97},{33,65},{65,33},{97,1},{2,98}... | collective-permute-start | bytes 196616 | tf_op jit(solution)/shard_map/ppermute | solution.py:343
  186.5 0.0 collective-permute-done.5.before_ref
  186.5 0.0 copy-start.4
  186.5 0.0 collective-permute-done.6.after_ref
  186.6 0.0 copy-start.5
  186.6 5.3 %collective-permute-done.11.z2_ref = bf16[128,256]{1,0:T(8,128)(2,1)S(1)} collective-permute-done((bf16[128,256]{1,0:T(8,128)(2,1)}, bf16[128,256]{1,0:T(8,128)(2,1)S(1)}, u32[]{:S(2)}, u32[]{:S(2)}) %collective-permute-start.11) | collective-permute-done | bytes 65568 | tf_op jit(solution)/shard_map/ppermute | solution.py:343
  191.9 11.1 %collective-permute-done.12.z3_ref = bf16[128,256]{1,0:T(8,128)(2,1)S(1)} collective-permute-done((bf16[128,256]{1,0:T(8,128)(2,1)}, bf16[128,256]{1,0:T(8,128)(2,1)S(1)}, u32[]{:S(2)}, u32[]{:S(2)}) %collective-permute-start.12) | collective-permute-done | bytes 65568 | tf_op jit(solution)/shard_map/ppermute | solution.py:343
  202.9 0.0 collective-permute-done.10.z1_ref
  203.0 0.0 copy-done.5
  203.0 0.0 copy-done.9
  203.0 0.6 copy-done.10
  203.6 0.1 copy-done.7
  203.6 3.3 %shard_map.82 = bf16[2048,256]{1,0:T(8,128)(2,1)} custom-call(f32[2048,256]{1,0:T(8,128)} %get-tuple-element.32.d_ref, bf16[256,256]{1,0:T(8,128)(2,1)} %copy-done.4, bf16[256,256]{1,0:T(8,128)(2,1)} %copy-done.5, bf16[256,256]{1,0:T(8,128)(2,1)} %copy-done.7, bf16[128,256]{1,0:T(8,128)(2,1)} %copy-done.9, bf16[128,256]{1,0:T(8,128)(2,1)} %copy-done.10, ...), custom_call_target="tpu_custom_call" | custom-call | bytes 5373952 | tf_op jit(solution)/shard_map/pallas_call | solution.py:316
  207.0 0.0 all-to-all-done.2.x_ref
  207.0 7.3 %all-to-all-start.3 = ((bf16[32,64,256]{2,1,0:T(8,128)(2,1)}), bf16[32,64,256]{2,1,0:T(8,128)(2,1)S(1)}, u32[]{:S(2)}, u32[]{:S(2)}) async-start(bf16[32,64,256]{2,1,0:T(8,128)(2,1)} %bitcast.10), calls=%async_computation.3 | async-start | bytes 2097152 | tf_op jit(solution)/shard_map/all_to_all | solution.py:336
  214.3 2.5 %shard_map.80 = (bf16[64,4096]{1,0:T(8,128)(2,1)}, bf16[64,4096]{1,0:T(8,128)(2,1)}) custom-call(bf16[32,64,256]{2,1,0:T(8,128)(2,1)} %copy-done.1), custom_call_target="tpu_custom_call" | custom-call | bytes 2097152 | tf_op jit(solution)/shard_map/pallas_call | solution.py:316
  216.7 24.2 %all-to-all-done.3.x_ref = bf16[32,64,256]{2,1,0:T(8,128)(2,1)S(1)} async-done(((bf16[32,64,256]{2,1,0:T(8,128)(2,1)}), bf16[32,64,256]{2,1,0:T(8,128)(2,1)S(1)}, u32[]{:S(2)}, u32[]{:S(2)}) %all-to-all-start.3) | async-done | bytes 1048608 | tf_op jit(solution)/shard_map/all_to_all | solution.py:336
  240.9 1.0 copy-done.2
  241.9 2.5 %shard_map.83 = (bf16[64,4096]{1,0:T(8,128)(2,1)}, bf16[64,4096]{1,0:T(8,128)(2,1)}) custom-call(bf16[32,64,256]{2,1,0:T(8,128)(2,1)} %copy-done.2), custom_call_target="tpu_custom_call" | custom-call | bytes 2097152 | tf_op jit(solution)/shard_map/pallas_call | solution.py:316
  (25 shorter events, 0.0 us)
Async XLA Ops:
  3.0 37.2 %all-to-all-start = ((bf16[32,64,256]{2,1,0:T(8,128)(2,1)}), bf16[32,64,256]{2,1,0:T(8,128)(2,1)S(1)}, u32[]{:S(2)}, u32[]{:S(2)}) async-start(bf16[32,64,256]{2,1,0:T(8,128)(2,1)} %shard_map.75), calls=%async_computation | async-start | bytes 2097152 | tf_op jit(solution)/shard_map/all_to_all | solution.py:336
  40.2 5.0 %copy-start = (bf16[32,64,256]{2,1,0:T(8,128)(2,1)}, bf16[32,64,256]{2,1,0:T(8,128)(2,1)S(1)}, u32[]{:S(2)}) copy-start(bf16[32,64,256]{2,1,0:T(8,128)(2,1)S(1)} %all-to-all-done) | copy-start | bytes 3145732
  40.2 59.0 %all-to-all-start.1 = ((bf16[32,64,256]{2,1,0:T(8,128)(2,1)}), bf16[32,64,256]{2,1,0:T(8,128)(2,1)S(1)}, u32[]{:S(2)}, u32[]{:S(2)}) async-start(bf16[32,64,256]{2,1,0:T(8,128)(2,1)} %shard_map.76), calls=%async_computation.1 | async-start | bytes 2097152 | tf_op jit(solution)/shard_map/all_to_all | solution.py:336
  47.9 26.9 %collective-permute-start.4 = (bf16[128,256]{1,0:T(8,128)(2,1)}, bf16[128,256]{1,0:T(8,128)(2,1)S(1)}, u32[]{:S(2)}, u32[]{:S(2)}) collective-permute-start(bf16[128,256]{1,0:T(8,128)(2,1)} %get-tuple-element.28.l4_ref), channel_id=1, source_target_pairs={{0,96},{32,64},{64,32},{96,0},{1,97},{33,65},{65,33},{97,1},{2,98}... | collective-permute-start | bytes 196616 | tf_op jit(solution)/shard_map/ppermute | solution.py:343
  57.2 23.6 %collective-permute-start.3 = (bf16[128,256]{1,0:T(8,128)(2,1)}, bf16[128,256]{1,0:T(8,128)(2,1)S(1)}, u32[]{:S(2)}, u32[]{:S(2)}) collective-permute-start(bf16[128,256]{1,0:T(8,128)(2,1)} %get-tuple-element.28.l4_ref), channel_id=1, source_target_pairs={{0,64},{32,96},{64,0},{96,32},{1,65},{33,97},{65,1},{97,33},{2,66}... | collective-permute-start | bytes 196616 | tf_op jit(solution)/shard_map/ppermute | solution.py:343
  63.2 19.5 %collective-permute-start.2 = (bf16[256,256]{1,0:T(8,128)(2,1)}, bf16[256,256]{1,0:T(8,128)(2,1)S(1)}, u32[]{:S(2)}, u32[]{:S(2)}) collective-permute-start(bf16[256,256]{1,0:T(8,128)(2,1)} %get-tuple-element.27), channel_id=1, source_target_pairs={{0,32},{32,0},{64,96},{96,64},{1,33},{33,1},{65,97},{97,65},{2,34}... | collective-permute-start | bytes 393224 | tf_op jit(solution)/shard_map/ppermute | solution.py:343
  67.1 32.1 %collective-permute-start = (bf16[256,256]{1,0:T(8,128)(2,1)S(1)}, bf16[256,256]{1,0:T(8,128)(2,1)S(1)}, u32[]{:S(2)}, u32[]{:S(2)}) collective-permute-start(bf16[256,256]{1,0:T(8,128)(2,1)S(1)} %bitcast.15), channel_id=1, source_target_pairs={{0,32},{32,64},{64,96},{96,128},{128,160},{160,192},{192,224},{224... | collective-permute-start | bytes 393224 | tf_op jit(solution)/shard_map/ppermute | solution.py:340
  73.4 25.8 %collective-permute-start.1 = (bf16[256,256]{1,0:T(8,128)(2,1)S(1)}, bf16[256,256]{1,0:T(8,128)(2,1)S(1)}, u32[]{:S(2)}, u32[]{:S(2)}) collective-permute-start(bf16[256,256]{1,0:T(8,128)(2,1)S(1)} %bitcast.14), channel_id=1, source_target_pairs={{32,0},{64,32},{96,64},{128,96},{160,128},{192,160},{224,192},{256... | collective-permute-start | bytes 393224 | tf_op jit(solution)/shard_map/ppermute | solution.py:340
  74.8 7.9 %copy-start.11 = (bf16[128,256]{1,0:T(8,128)(2,1)}, bf16[128,256]{1,0:T(8,128)(2,1)S(1)}, u32[]{:S(2)}) copy-start(bf16[128,256]{1,0:T(8,128)(2,1)S(1)} %collective-permute-done.4.z3_ref) | copy-start | bytes 196612
  80.8 1.9 copy-start.12
  82.7 0.7 copy-start.6
  99.3 1.0 copy-start.3
  99.3 1.0 copy-start.17
  99.3 1.1 copy-start.19
  124.6 24.6 %copy-start.18 = (bf16[256,256]{1,0:T(8,128)(2,1)S(1)}, bf16[256,256]{1,0:T(8,128)(2,1)}, u32[]{:S(2)}) copy-start(bf16[256,256]{1,0:T(8,128)(2,1)} %get-tuple-element.35) | copy-start | bytes 393220
  124.6 26.6 %copy-start.21 = (bf16[128,256]{1,0:T(8,128)(2,1)S(1)}, bf16[128,256]{1,0:T(8,128)(2,1)}, u32[]{:S(2)}) copy-start(bf16[128,256]{1,0:T(8,128)(2,1)} %get-tuple-element.36) | copy-start | bytes 196612
  124.6 30.9 %copy-start.20 = (bf16[128,256]{1,0:T(8,128)(2,1)S(1)}, bf16[128,256]{1,0:T(8,128)(2,1)}, u32[]{:S(2)}) copy-start(bf16[128,256]{1,0:T(8,128)(2,1)} %get-tuple-element.37) | copy-start | bytes 196612
  124.6 34.2 %copy-start.16 = (bf16[256,256]{1,0:T(8,128)(2,1)S(1)}, bf16[256,256]{1,0:T(8,128)(2,1)}, u32[]{:S(2)}) copy-start(bf16[256,256]{1,0:T(8,128)(2,1)} %get-tuple-element.33) | copy-start | bytes 393220
  124.6 41.0 %copy-start.15 = (bf16[256,256]{1,0:T(8,128)(2,1)S(1)}, bf16[256,256]{1,0:T(8,128)(2,1)}, u32[]{:S(2)}) copy-start(bf16[256,256]{1,0:T(8,128)(2,1)} %get-tuple-element.34) | copy-start | bytes 393220
  124.6 82.3 %all-to-all-start.2 = ((bf16[32,64,256]{2,1,0:T(8,128)(2,1)}), bf16[32,64,256]{2,1,0:T(8,128)(2,1)S(1)}, u32[]{:S(2)}, u32[]{:S(2)}) async-start(bf16[32,64,256]{2,1,0:T(8,128)(2,1)} %bitcast.11), calls=%async_computation.2 | async-start | bytes 2097152 | tf_op jit(solution)/shard_map/all_to_all | solution.py:336
  149.2 17.8 %collective-permute-start.7 = (bf16[256,256]{1,0:T(8,128)(2,1)S(1)}, bf16[256,256]{1,0:T(8,128)(2,1)S(1)}, u32[]{:S(2)}, u32[]{:S(2)}) collective-permute-start(bf16[256,256]{1,0:T(8,128)(2,1)S(1)} %copy-done.18), channel_id=1, source_target_pairs={{0,128},{128,0},{256,384},{384,256},{1,129},{129,1},{257,385},{385... | collective-permute-start | bytes 393224 | tf_op jit(solution)/shard_map/ppermute | solution.py:343
  151.2 15.8 %collective-permute-start.8 = (bf16[128,256]{1,0:T(8,128)(2,1)S(1)}, bf16[128,256]{1,0:T(8,128)(2,1)S(1)}, u32[]{:S(2)}, u32[]{:S(2)}) collective-permute-start(bf16[128,256]{1,0:T(8,128)(2,1)S(1)} %copy-done.21), channel_id=1, source_target_pairs={{0,256},{128,384},{256,0},{384,128},{1,257},{129,385},{257,1},{385... | collective-permute-start | bytes 196616 | tf_op jit(solution)/shard_map/ppermute | solution.py:343
  155.5 11.5 %collective-permute-start.9 = (bf16[128,256]{1,0:T(8,128)(2,1)S(1)}, bf16[128,256]{1,0:T(8,128)(2,1)S(1)}, u32[]{:S(2)}, u32[]{:S(2)}) collective-permute-start(bf16[128,256]{1,0:T(8,128)(2,1)S(1)} %copy-done.20), channel_id=1, source_target_pairs={{0,384},{128,256},{256,128},{384,0},{1,385},{129,257},{257,129},{3... | collective-permute-start | bytes 196616 | tf_op jit(solution)/shard_map/ppermute | solution.py:343
  158.9 27.6 %collective-permute-start.5 = (bf16[256,256]{1,0:T(8,128)(2,1)S(1)}, bf16[256,256]{1,0:T(8,128)(2,1)S(1)}, u32[]{:S(2)}, u32[]{:S(2)}) collective-permute-start(bf16[256,256]{1,0:T(8,128)(2,1)S(1)} %copy-done.16), channel_id=1, source_target_pairs={{0,32},{32,64},{64,96},{96,128},{128,160},{160,192},{192,224},{224... | collective-permute-start | bytes 393224 | tf_op jit(solution)/shard_map/ppermute | solution.py:340
  165.7 20.9 %collective-permute-start.6 = (bf16[256,256]{1,0:T(8,128)(2,1)S(1)}, bf16[256,256]{1,0:T(8,128)(2,1)S(1)}, u32[]{:S(2)}, u32[]{:S(2)}) collective-permute-start(bf16[256,256]{1,0:T(8,128)(2,1)S(1)} %copy-done.15), channel_id=1, source_target_pairs={{32,0},{64,32},{96,64},{128,96},{160,128},{192,160},{224,192},{256... | collective-permute-start | bytes 393224 | tf_op jit(solution)/shard_map/ppermute | solution.py:340
  167.0 0.6 copy-start.13
  167.0 0.6 copy-start.14
  167.0 0.7 copy-start.8
  169.7 33.3 %collective-permute-start.10 = (bf16[256,256]{1,0:T(8,128)(2,1)}, bf16[256,256]{1,0:T(8,128)(2,1)S(1)}, u32[]{:S(2)}, u32[]{:S(2)}) collective-permute-start(bf16[256,256]{1,0:T(8,128)(2,1)} %get-tuple-element.40), channel_id=1, source_target_pairs={{0,32},{32,0},{64,96},{96,64},{1,33},{33,1},{65,97},{97,65},{2,34}... | collective-permute-start | bytes 393224 | tf_op jit(solution)/shard_map/ppermute | solution.py:343
  177.6 14.3 %collective-permute-start.11 = (bf16[128,256]{1,0:T(8,128)(2,1)}, bf16[128,256]{1,0:T(8,128)(2,1)S(1)}, u32[]{:S(2)}, u32[]{:S(2)}) collective-permute-start(bf16[128,256]{1,0:T(8,128)(2,1)} %get-tuple-element.41), channel_id=1, source_target_pairs={{0,64},{32,96},{64,0},{96,32},{1,65},{33,97},{65,1},{97,33},{2,66}... | collective-permute-start | bytes 196616 | tf_op jit(solution)/shard_map/ppermute | solution.py:343
  181.9 21.1 %collective-permute-start.12 = (bf16[128,256]{1,0:T(8,128)(2,1)}, bf16[128,256]{1,0:T(8,128)(2,1)S(1)}, u32[]{:S(2)}, u32[]{:S(2)}) collective-permute-start(bf16[128,256]{1,0:T(8,128)(2,1)} %get-tuple-element.42), channel_id=1, source_target_pairs={{0,96},{32,64},{64,32},{96,0},{1,97},{33,65},{65,33},{97,1},{2,98}... | collective-permute-start | bytes 196616 | tf_op jit(solution)/shard_map/ppermute | solution.py:343
  186.5 16.4 %copy-start.4 = (bf16[256,256]{1,0:T(8,128)(2,1)}, bf16[256,256]{1,0:T(8,128)(2,1)S(1)}, u32[]{:S(2)}) copy-start(bf16[256,256]{1,0:T(8,128)(2,1)S(1)} %collective-permute-done.5.before_ref) | copy-start | bytes 393220
  186.6 16.4 %copy-start.5 = (bf16[256,256]{1,0:T(8,128)(2,1)}, bf16[256,256]{1,0:T(8,128)(2,1)S(1)}, u32[]{:S(2)}) copy-start(bf16[256,256]{1,0:T(8,128)(2,1)S(1)} %collective-permute-done.6.after_ref) | copy-start | bytes 393220
  191.9 11.1 %copy-start.9 = (bf16[128,256]{1,0:T(8,128)(2,1)}, bf16[128,256]{1,0:T(8,128)(2,1)S(1)}, u32[]{:S(2)}) copy-start(bf16[128,256]{1,0:T(8,128)(2,1)S(1)} %collective-permute-done.11.z2_ref) | copy-start | bytes 196612
  202.9 0.6 copy-start.10
  202.9 0.7 copy-start.7
  207.0 7.3 %copy-start.1 = (bf16[32,64,256]{2,1,0:T(8,128)(2,1)}, bf16[32,64,256]{2,1,0:T(8,128)(2,1)S(1)}, u32[]{:S(2)}) copy-start(bf16[32,64,256]{2,1,0:T(8,128)(2,1)S(1)} %all-to-all-done.2.x_ref) | copy-start | bytes 3145732
  207.0 34.0 %all-to-all-start.3 = ((bf16[32,64,256]{2,1,0:T(8,128)(2,1)}), bf16[32,64,256]{2,1,0:T(8,128)(2,1)S(1)}, u32[]{:S(2)}, u32[]{:S(2)}) async-start(bf16[32,64,256]{2,1,0:T(8,128)(2,1)} %bitcast.10), calls=%async_computation.3 | async-start | bytes 2097152 | tf_op jit(solution)/shard_map/all_to_all | solution.py:336
  240.9 1.0 copy-start.2

commit v3 on v2

--- a/solution.py
+++ b/solution.py
@@ -25,6 +25,8 @@
 SIB = [0, 0, 1024, 1536, 1792, 2048, 2304]
 SIB_ROWS = 2560
 
+PARTS = 4
+
 VMEM = pl.BlockSpec(memory_space=pltpu.VMEM)
 SMEM = pl.BlockSpec(memory_space=pltpu.SMEM)
 
@@ -82,10 +84,31 @@
         o_ref[h, :, HD : 2 * HD] = b_ref[:, h * HD : (h + 1) * HD]
 
 
+def pack(a, b):
+    rows, width = a.shape
+    return call(pack_kernel, shape(bf16, width // HD, rows, 2 * HD), 0, (a, b))
+
+
 def unpack_kernel(x_ref, a_ref, b_ref):
-    for h in range(x_ref.shape[0]):
-        a_ref[:, h * HD : (h + 1) * HD] = x_ref[h, :, 0:HD]
-        b_ref[:, h * HD : (h + 1) * HD] = x_ref[h, :, HD : 2 * HD]
+    i = pl.program_id(0)
+    n = x_ref.shape[0] // PARTS
+    for h in range(n):
+        a_ref[:, h * HD : (h + 1) * HD] = x_ref[i * n + h, :, 0:HD]
+        b_ref[:, h * HD : (h + 1) * HD] = x_ref[i * n + h, :, HD : 2 * HD]
+
+
+def unpack(x):
+    heads, rows, _ = x.shape
+    width = heads * HD
+    part = pl.BlockSpec((rows, width // PARTS), lambda i: (0, i))
+    return pl.pallas_call(
+        unpack_kernel,
+        grid=(PARTS,),
+        out_shape=(shape(bf16, rows, width), shape(bf16, rows, width)),
+        in_specs=[VMEM],
+        out_specs=(part, part),
+        cost_estimate=pl.CostEstimate(flops=0, bytes_accessed=4 * x.size, transcendentals=0),
+    )(pltpu.with_memory_space_constraint(x, pltpu.VMEM))
 
 
 def levels_kernel(kv_ref, l1_ref, l2_ref, l3_ref, l4_ref):
@@ -262,7 +285,8 @@
         j = b // 2
         src = pl.multiple_of(SIB[1] + (j + 1 - 2 * (j % 2)) * BLOCK + (b % 2) * half, half)
         own = pl.ds(pl.multiple_of((b + 1) * BLOCK, BLOCK), BLOCK)
-        d_ref[rows, :] = gkx[own, :] + rep_pair(gs[pl.ds(src, half), :] * 0.5, tmp.at[1], tmp.at[2])
+        local = gkx[own, :] + rep_pair(gs[pl.ds(src, half), :] * 0.5, tmp.at[1], tmp.at[2])
+        d_ref[rows, :] = local.astype(bf16)
         return carry
 
     lax.fori_loop(0, CHUNK_BLOCKS, finish, 0)
@@ -299,7 +323,7 @@
     for b in range(4):
         b_s[b * BLOCK : (b + 1) * BLOCK, :] = rep2(a_s[b * half : (b + 1) * half, :])
     for b in range(8):
-        total = d_ref[b * BLOCK : (b + 1) * BLOCK, :] + rep2(b_s[b * half : (b + 1) * half, :])
+        total = d_ref[b * BLOCK : (b + 1) * BLOCK, :].astype(f32) + rep2(b_s[b * half : (b + 1) * half, :])
         if b == 0:
             total = total + before_ref[...].astype(f32)
         if b == 7:
@@ -311,7 +335,8 @@
     return jax.ShapeDtypeStruct(dims, dtype)
 
 
-def call(kernel, out_shape, scalars, args, scratch=(), flops=0):
+def call(kernel, out_shape, scalars, args, scratch=(), flops=0, near=()):
+    args = [pltpu.with_memory_space_constraint(a, pltpu.VMEM) if i in near else a for i, a in enumerate(args)]
     nbytes = sum(a.size * a.dtype.itemsize for a in args)
     return pl.pallas_call(
         kernel,
@@ -329,9 +354,6 @@
     chunk = (lax.axis_index("y") * lax.axis_size("zh") + lax.axis_index("zh")).astype(jnp.int32).reshape(1)
     wide = 2 * HD
 
-    def pack(a, b):
-        return call(pack_kernel, shape(bf16, heads, own_rows, wide), 0, (a, b))
-
     def swap(x):
         return lax.all_to_all(x, ("zl", "h"), split_axis=0, concat_axis=0, tiled=True)
 
@@ -348,6 +370,7 @@
         (shape(bf16, 1024, wide), shape(bf16, 512, wide), shape(bf16, 256, wide), shape(bf16, 128, wide)),
         0,
         (kv,),
+        near=(0,),
     )
     z1, z2, z3 = flip(l3, "zh", 1), flip(l4, "zh", 2), flip(l4, "zh", 3)
     before = shift(kv[ROWS - BLOCK :], 1)
@@ -360,7 +383,7 @@
         main_kernel,
         (
             shape(bf16, ROWS, wide),
-            shape(f32, ROWS, wide),
+            shape(bf16, ROWS, wide),
             shape(bf16, BLOCK, wide),
             shape(bf16, BLOCK, wide),
             shape(f32, BLOCK, wide),
@@ -386,21 +409,23 @@
             coarse,
             coarse,
             pltpu.VMEM((ROWS, HD), f32),
-            pltpu.VMEM((5, BLOCK, HD), f32),
+            pltpu.VMEM((5, BLOCK + 8, HD), f32),
         ),
         flops=4_000_000_000,
+        near=(2,),
     )
     out_ag = swap(ag.reshape(heads, own_rows, wide))
     r1, r2, r3 = flip(t1, "y", 1), flip(t2, "y", 2), flip(t3, "y", 3)
     before = shift(up, 1)
     after = shift(down, -1)
-    two = pltpu.VMEM((2, BLOCK, HD), f32)
+    two = pltpu.VMEM((2, BLOCK + 8, HD), f32)
     own5, w1, w2, w3 = call(
         fold_kernel,
         (shape(f32, 64, wide), shape(bf16, BLOCK, wide), shape(bf16, 128, wide), shape(bf16, 128, wide)),
         0,
         (r1, r2, r3, w1, w2),
         scratch=(two,),
+        near=(0, 1, 2),
     )
     z1, z2, z3 = flip(w1, "zh", 1), flip(w2, "zh", 2), flip(w3, "zh", 3)
     gkv = call(
@@ -409,11 +434,11 @@
         0,
         (d, before, after, z1, z2, z3, own5),
         scratch=(two, pltpu.VMEM((512, wide), f32), pltpu.VMEM((1024, wide), f32)),
+        near=(1, 2, 3, 4, 5),
     )
     out_kv = swap(gkv.reshape(heads, own_rows, wide))
-    pair = (shape(bf16, own_rows, width), shape(bf16, own_rows, width))
-    attended, grad_query = call(unpack_kernel, pair, 0, (out_ag,))
-    grad_key, grad_value = call(unpack_kernel, pair, 0, (out_kv,))
+    attended, grad_query = unpack(out_ag)
+    grad_key, grad_value = unpack(out_kv)
     return attended, grad_query, grad_key, grad_value
 
 

time: 246 us -> 241 us (0.980)
  Pallas kernels: 43.9 us -> 39.6 us
  local copies, waits for them, and re-layouts: 5.07 us -> 1.96 us
    pallas_call x9 -> x7, Pallas kernels: 43.9 us -> 36.3 us  [call(): pl.pallas_call(kernel, out_shape=out_shape, in_specs=[SMEM] * scalars + [...]
    pallas_call x0 -> x2, Pallas kernels: none -> 3.26 us  [unpack(): pl.pallas_call(unpack_kernel, grid=(PARTS,), out_shape=(shape(bf16, rows,...]
  transfers between devices with their start and end apart: 17 -> 17, of which waited for: 7 -> 6; matrix products, arithmetic and copies ran while one was open for 0% -> 0% of each run, Pallas kernels for 6% -> 5%
where the time goes in v3:
time: 241 us; the launch traced here: 240 us
  starting transfers between devices  110 us (46%)
  waiting for transfers between devices  74.7 us (31%)
  Pallas kernels  39.6 us (16%)
  blocking collectives  12.8 us (5%)
    all_to_all x4, starting transfers between devices, swap(): lax.all_to_all(x, ('zl', 'h'), split_axis=0, concat_axis=0, tiled=True)  49.7 us
    all_to_all x4, waiting for transfers between devices, swap(): lax.all_to_all(x, ('zl', 'h'), split_axis=0, concat_axis=0, tiled=True)  49.4 us
    ppermute x9, starting transfers between devices, flip(): return lax.ppermute(x, axis, [(i, i ^ bits) for i in range(4)])  44.6 us
    pallas_call x7, Pallas kernels, call(): pl.pallas_call(kernel, out_shape=out_shape, in_specs=[SMEM] * scalars + [...  36.3 us
    ppermute x9, waiting for transfers between devices, flip(): return lax.ppermute(x, axis, [(i, i ^ bits) for i in range(4)])  25.3 us
    ppermute x4, starting transfers between devices, shift(): return lax.ppermute(x, ('y', 'zh'), pairs)  15.7 us
    all_gather x1, blocking collectives, per_device(): far = lax.all_gather(group, 'y')  12.8 us
  transfers between devices with their start and end apart: 17, of which 6 were waited for; matrix products, arithmetic and copies ran while one was open for 0% of the time, Pallas kernels for 5%

profile of v3, /device:TPU:1, one launch (start us, length us, event | category | flops | bytes accessed | tf_op | source)
XLA Modules:
  0.0 240.0 jit_solution(10756457051780242572)
XLA Ops:
  0.6 2.3 shard_map.75
  3.0 10.4 %all-to-all-start = ((bf16[32,64,256]{2,1,0:T(8,128)(2,1)}), bf16[32,64,256]{2,1,0:T(8,128)(2,1)S(1)}, u32[]{:S(2)}, u32[]{:S(2)}) async-start(bf16[32,64,256]{2,1,0:T(8,128)(2,1)} %shard_map.75), calls=%async_computation | async-start | bytes 2097152 | tf_op jit(solution)/shard_map/all_to_all | solution.py:358
  13.4 2.4 shard_map.76
  15.8 24.4 %all-to-all-done = bf16[32,64,256]{2,1,0:T(8,128)(2,1)S(1)} async-done(((bf16[32,64,256]{2,1,0:T(8,128)(2,1)}), bf16[32,64,256]{2,1,0:T(8,128)(2,1)S(1)}, u32[]{:S(2)}, u32[]{:S(2)}) %all-to-all-start) | async-done | bytes 1048608 | tf_op jit(solution)/shard_map/all_to_all | solution.py:358
  40.2 0.0 copy-start
  40.2 5.0 %all-to-all-start.1 = ((bf16[32,64,256]{2,1,0:T(8,128)(2,1)}), bf16[32,64,256]{2,1,0:T(8,128)(2,1)S(1)}, u32[]{:S(2)}, u32[]{:S(2)}) async-start(bf16[32,64,256]{2,1,0:T(8,128)(2,1)} %shard_map.76), calls=%async_computation.1 | async-start | bytes 2097152 | tf_op jit(solution)/shard_map/all_to_all | solution.py:358
  45.2 1.4 shard_map.77
  46.6 9.3 %collective-permute-start.4 = (bf16[128,256]{1,0:T(8,128)(2,1)}, bf16[128,256]{1,0:T(8,128)(2,1)S(1)}, u32[]{:S(2)}, u32[]{:S(2)}) collective-permute-start(bf16[128,256]{1,0:T(8,128)(2,1)} %get-tuple-element.28.l4_ref), channel_id=1, source_target_pairs={{0,96},{32,64},{64,32},{96,0},{1,97},{33,65},{65,33},{97,1},{2,98}... | collective-permute-start | bytes 196616 | tf_op jit(solution)/shard_map/ppermute | solution.py:365
  55.9 6.1 %collective-permute-start.3 = (bf16[128,256]{1,0:T(8,128)(2,1)}, bf16[128,256]{1,0:T(8,128)(2,1)S(1)}, u32[]{:S(2)}, u32[]{:S(2)}) collective-permute-start(bf16[128,256]{1,0:T(8,128)(2,1)} %get-tuple-element.28.l4_ref), channel_id=1, source_target_pairs={{0,64},{32,96},{64,0},{96,32},{1,65},{33,97},{65,1},{97,33},{2,66}... | collective-permute-start | bytes 196616 | tf_op jit(solution)/shard_map/ppermute | solution.py:365
  62.0 2.9 %collective-permute-start.2 = (bf16[256,256]{1,0:T(8,128)(2,1)}, bf16[256,256]{1,0:T(8,128)(2,1)S(1)}, u32[]{:S(2)}, u32[]{:S(2)}) collective-permute-start(bf16[256,256]{1,0:T(8,128)(2,1)} %get-tuple-element.27), channel_id=1, source_target_pairs={{0,32},{32,0},{64,96},{96,64},{1,33},{33,1},{65,97},{97,65},{2,34}... | collective-permute-start | bytes 393224 | tf_op jit(solution)/shard_map/ppermute | solution.py:365
  64.8 0.0 copy-done
  64.9 6.3 %collective-permute-start = (bf16[256,256]{1,0:T(8,128)(2,1)S(1)}, bf16[256,256]{1,0:T(8,128)(2,1)S(1)}, u32[]{:S(2)}, u32[]{:S(2)}) collective-permute-start(bf16[256,256]{1,0:T(8,128)(2,1)S(1)} %bitcast.15), channel_id=1, source_target_pairs={{0,32},{32,64},{64,96},{96,128},{128,160},{160,192},{192,224},{224... | collective-permute-start | bytes 393224 | tf_op jit(solution)/shard_map/ppermute | solution.py:362
  71.2 1.3 collective-permute-start.1
  72.5 1.6 collective-permute-done.4.z3_ref
  74.1 0.0 copy-start.2
  74.1 6.4 %collective-permute-done.3.z2_ref = bf16[128,256]{1,0:T(8,128)(2,1)S(1)} collective-permute-done((bf16[128,256]{1,0:T(8,128)(2,1)}, bf16[128,256]{1,0:T(8,128)(2,1)S(1)}, u32[]{:S(2)}, u32[]{:S(2)}) %collective-permute-start.3) | collective-permute-done | bytes 65568 | tf_op jit(solution)/shard_map/ppermute | solution.py:365
  80.5 0.0 collective-permute-done.2.z1_ref
  80.5 0.0 copy-done.2
  80.5 0.6 copy-done.3
  81.1 0.0 copy-start.1
  81.1 0.6 copy-done.1
  81.8 2.0 shard_map.78
  83.7 12.8 %all-gather = bf16[1024,256]{1,0:T(8,128)(2,1)} all-gather(bf16[256,256]{1,0:T(8,128)(2,1)} %shard_map.78), channel_id=2, replica_groups=mesh['y'=4,'zh'=4,'zl'=4,'h'=8] {'y'}, dimensions={0}, use_global_device_ids=true | all-gather | bytes 655360 | tf_op jit(solution)/shard_map/all_gather | solution.py:380
  96.6 0.0 all-to-all-done.1
  96.6 0.0 collective-permute-done.before_ref
  96.6 0.0 copy-start.6
  96.6 0.0 collective-permute-done.1.after_ref
  96.6 0.0 copy-start.8
  96.6 0.6 copy-done.6
  97.2 0.1 copy-done.8
  97.3 23.6 %shard_map.79 = (bf16[2048,256]{1,0:T(8,128)(2,1)}, bf16[2048,256]{1,0:T(8,128)(2,1)}, bf16[256,256]{1,0:T(8,128)(2,1)}, bf16[256,256]{1,0:T(8,128)(2,1)}, f32[2...) custom-call(s32[1]{0:T(128)} %bitcast.c_ref, ...), custom_call_target="tpu_custom_call" | custom-call | flops 4000000000 | bytes 7864328 | tf_op jit(solution)/shard_map/pallas_call | solution.py:341
  120.8 0.0 copy-start.7
  120.8 0.0 copy-start.9
  120.9 0.0 copy-start.5
  120.9 0.0 copy-start.4
  120.9 27.2 %all-to-all-start.2 = ((bf16[32,64,256]{2,1,0:T(8,128)(2,1)}), bf16[32,64,256]{2,1,0:T(8,128)(2,1)S(1)}, u32[]{:S(2)}, u32[]{:S(2)}) async-start(bf16[32,64,256]{2,1,0:T(8,128)(2,1)} %bitcast.12), calls=%async_computation.2 | async-start | bytes 2097152 | tf_op jit(solution)/shard_map/all_to_all | solution.py:358
  148.1 0.0 copy-done.7
  148.1 2.0 collective-permute-start.7
  150.1 0.0 copy-done.10
  150.1 4.3 %collective-permute-start.8 = (bf16[128,256]{1,0:T(8,128)(2,1)S(1)}, bf16[128,256]{1,0:T(8,128)(2,1)S(1)}, u32[]{:S(2)}, u32[]{:S(2)}) collective-permute-start(bf16[128,256]{1,0:T(8,128)(2,1)S(1)} %copy-done.10), channel_id=1, source_target_pairs={{0,256},{128,384},{256,0},{384,128},{1,257},{129,385},{257,1},{385... | collective-permute-start | bytes 196616 | tf_op jit(solution)/shard_map/ppermute | solution.py:365
  154.4 0.0 copy-done.9
  154.4 3.3 %collective-permute-start.9 = (bf16[128,256]{1,0:T(8,128)(2,1)S(1)}, bf16[128,256]{1,0:T(8,128)(2,1)S(1)}, u32[]{:S(2)}, u32[]{:S(2)}) collective-permute-start(bf16[128,256]{1,0:T(8,128)(2,1)S(1)} %copy-done.9), channel_id=1, source_target_pairs={{0,384},{128,256},{256,128},{384,0},{1,385},{129,257},{257,129},{3... | collective-permute-start | bytes 196616 | tf_op jit(solution)/shard_map/ppermute | solution.py:365
  157.7 0.0 copy-done.5
  157.7 6.8 %collective-permute-start.5 = (bf16[256,256]{1,0:T(8,128)(2,1)S(1)}, bf16[256,256]{1,0:T(8,128)(2,1)S(1)}, u32[]{:S(2)}, u32[]{:S(2)}) collective-permute-start(bf16[256,256]{1,0:T(8,128)(2,1)S(1)} %copy-done.5), channel_id=1, source_target_pairs={{0,32},{32,64},{64,96},{96,128},{128,160},{160,192},{192,224},{224... | collective-permute-start | bytes 393224 | tf_op jit(solution)/shard_map/ppermute | solution.py:362
  164.5 0.0 copy-done.4
  164.5 1.3 collective-permute-start.6
  165.8 0.0 collective-permute-done.8.r2_ref
  165.8 0.0 collective-permute-done.9.r3_ref
  165.9 0.0 collective-permute-done.7.r1_ref
  165.9 1.8 shard_map.81
  167.7 7.9 %collective-permute-start.10 = (bf16[256,256]{1,0:T(8,128)(2,1)}, bf16[256,256]{1,0:T(8,128)(2,1)S(1)}, u32[]{:S(2)}, u32[]{:S(2)}) collective-permute-start(bf16[256,256]{1,0:T(8,128)(2,1)} %get-tuple-element.40), channel_id=1, source_target_pairs={{0,32},{32,0},{64,96},{96,64},{1,33},{33,1},{65,97},{97,65},{2,34}... | collective-permute-start | bytes 393224 | tf_op jit(solution)/shard_map/ppermute | solution.py:365
  175.6 4.3 %collective-permute-start.11 = (bf16[128,256]{1,0:T(8,128)(2,1)}, bf16[128,256]{1,0:T(8,128)(2,1)S(1)}, u32[]{:S(2)}, u32[]{:S(2)}) collective-permute-start(bf16[128,256]{1,0:T(8,128)(2,1)} %get-tuple-element.41), channel_id=1, source_target_pairs={{0,64},{32,96},{64,0},{96,32},{1,65},{33,97},{65,1},{97,33},{2,66}... | collective-permute-start | bytes 196616 | tf_op jit(solution)/shard_map/ppermute | solution.py:365
  179.9 4.7 %collective-permute-start.12 = (bf16[128,256]{1,0:T(8,128)(2,1)}, bf16[128,256]{1,0:T(8,128)(2,1)S(1)}, u32[]{:S(2)}, u32[]{:S(2)}) collective-permute-start(bf16[128,256]{1,0:T(8,128)(2,1)} %get-tuple-element.42), channel_id=1, source_target_pairs={{0,96},{32,64},{64,32},{96,0},{1,97},{33,65},{65,33},{97,1},{2,98}... | collective-permute-start | bytes 196616 | tf_op jit(solution)/shard_map/ppermute | solution.py:365
  184.5 0.0 collective-permute-done.5.before_ref
  184.5 0.0 collective-permute-done.6.after_ref
  184.6 5.4 %collective-permute-done.11.z2_ref = bf16[128,256]{1,0:T(8,128)(2,1)S(1)} collective-permute-done((bf16[128,256]{1,0:T(8,128)(2,1)}, bf16[128,256]{1,0:T(8,128)(2,1)S(1)}, u32[]{:S(2)}, u32[]{:S(2)}) %collective-permute-start.11) | collective-permute-done | bytes 65568 | tf_op jit(solution)/shard_map/ppermute | solution.py:365
  189.9 11.9 %collective-permute-done.12.z3_ref = bf16[128,256]{1,0:T(8,128)(2,1)S(1)} collective-permute-done((bf16[128,256]{1,0:T(8,128)(2,1)}, bf16[128,256]{1,0:T(8,128)(2,1)S(1)}, u32[]{:S(2)}, u32[]{:S(2)}) %collective-permute-start.12) | collective-permute-done | bytes 65568 | tf_op jit(solution)/shard_map/ppermute | solution.py:365
  201.8 0.0 collective-permute-done.10.z1_ref
  201.8 2.9 %shard_map.82 = bf16[2048,256]{1,0:T(8,128)(2,1)} custom-call(bf16[2048,256]{1,0:T(8,128)(2,1)} %get-tuple-element.32.d_ref, bf16[256,256]{1,0:T(8,128)(2,1)S(1)} %collective-permute-done.5.before_ref, bf16[256,256]{1,0:T(8,128)(2,1)S(1)} %collective-permute-done.6.after_ref, bf16[256,256]{1,0:T(8,128)(2,1)S(1)} %collective-permute-done.10.z1_ref, ...), custom_call_target="tpu_custom_call" | custom-call | bytes 3276800 | tf_op jit(solution)/shard_map/pallas_call | solution.py:341
  204.7 0.0 all-to-all-done.2.x_ref
  204.7 7.0 %all-to-all-start.3 = ((bf16[32,64,256]{2,1,0:T(8,128)(2,1)}), bf16[32,64,256]{2,1,0:T(8,128)(2,1)S(1)}, u32[]{:S(2)}, u32[]{:S(2)}) async-start(bf16[32,64,256]{2,1,0:T(8,128)(2,1)} %bitcast.11), calls=%async_computation.3 | async-start | bytes 2097152 | tf_op jit(solution)/shard_map/all_to_all | solution.py:358
  211.7 1.6 shard_map.80
  213.3 25.0 %all-to-all-done.3.x_ref = bf16[32,64,256]{2,1,0:T(8,128)(2,1)S(1)} async-done(((bf16[32,64,256]{2,1,0:T(8,128)(2,1)}), bf16[32,64,256]{2,1,0:T(8,128)(2,1)S(1)}, u32[]{:S(2)}, u32[]{:S(2)}) %all-to-all-start.3) | async-done | bytes 1048608 | tf_op jit(solution)/shard_map/all_to_all | solution.py:358
  238.4 1.6 shard_map.83
  (3 shorter events, 0.0 us)
Async XLA Ops:
  3.0 37.2 %all-to-all-start = ((bf16[32,64,256]{2,1,0:T(8,128)(2,1)}), bf16[32,64,256]{2,1,0:T(8,128)(2,1)S(1)}, u32[]{:S(2)}, u32[]{:S(2)}) async-start(bf16[32,64,256]{2,1,0:T(8,128)(2,1)} %shard_map.75), calls=%async_computation | async-start | bytes 2097152 | tf_op jit(solution)/shard_map/all_to_all | solution.py:358
  40.2 24.7 %copy-start = (bf16[32,64,256]{2,1,0:T(8,128)(2,1)}, bf16[32,64,256]{2,1,0:T(8,128)(2,1)S(1)}, u32[]{:S(2)}) copy-start(bf16[32,64,256]{2,1,0:T(8,128)(2,1)S(1)} %all-to-all-done) | copy-start | bytes 3145732
  40.2 56.4 %all-to-all-start.1 = ((bf16[32,64,256]{2,1,0:T(8,128)(2,1)}), bf16[32,64,256]{2,1,0:T(8,128)(2,1)S(1)}, u32[]{:S(2)}, u32[]{:S(2)}) async-start(bf16[32,64,256]{2,1,0:T(8,128)(2,1)} %shard_map.76), calls=%async_computation.1 | async-start | bytes 2097152 | tf_op jit(solution)/shard_map/all_to_all | solution.py:358
  46.6 27.5 %collective-permute-start.4 = (bf16[128,256]{1,0:T(8,128)(2,1)}, bf16[128,256]{1,0:T(8,128)(2,1)S(1)}, u32[]{:S(2)}, u32[]{:S(2)}) collective-permute-start(bf16[128,256]{1,0:T(8,128)(2,1)} %get-tuple-element.28.l4_ref), channel_id=1, source_target_pairs={{0,96},{32,64},{64,32},{96,0},{1,97},{33,65},{65,33},{97,1},{2,98}... | collective-permute-start | bytes 196616 | tf_op jit(solution)/shard_map/ppermute | solution.py:365
  55.9 24.6 %collective-permute-start.3 = (bf16[128,256]{1,0:T(8,128)(2,1)}, bf16[128,256]{1,0:T(8,128)(2,1)S(1)}, u32[]{:S(2)}, u32[]{:S(2)}) collective-permute-start(bf16[128,256]{1,0:T(8,128)(2,1)} %get-tuple-element.28.l4_ref), channel_id=1, source_target_pairs={{0,64},{32,96},{64,0},{96,32},{1,65},{33,97},{65,1},{97,33},{2,66}... | collective-permute-start | bytes 196616 | tf_op jit(solution)/shard_map/ppermute | solution.py:365
  62.0 18.5 %collective-permute-start.2 = (bf16[256,256]{1,0:T(8,128)(2,1)}, bf16[256,256]{1,0:T(8,128)(2,1)S(1)}, u32[]{:S(2)}, u32[]{:S(2)}) collective-permute-start(bf16[256,256]{1,0:T(8,128)(2,1)} %get-tuple-element.27), channel_id=1, source_target_pairs={{0,32},{32,0},{64,96},{96,64},{1,33},{33,1},{65,97},{97,65},{2,34}... | collective-permute-start | bytes 393224 | tf_op jit(solution)/shard_map/ppermute | solution.py:365
  64.9 31.7 %collective-permute-start = (bf16[256,256]{1,0:T(8,128)(2,1)S(1)}, bf16[256,256]{1,0:T(8,128)(2,1)S(1)}, u32[]{:S(2)}, u32[]{:S(2)}) collective-permute-start(bf16[256,256]{1,0:T(8,128)(2,1)S(1)} %bitcast.15), channel_id=1, source_target_pairs={{0,32},{32,64},{64,96},{96,128},{128,160},{160,192},{192,224},{224... | collective-permute-start | bytes 393224 | tf_op jit(solution)/shard_map/ppermute | solution.py:362
  71.2 25.4 %collective-permute-start.1 = (bf16[256,256]{1,0:T(8,128)(2,1)S(1)}, bf16[256,256]{1,0:T(8,128)(2,1)S(1)}, u32[]{:S(2)}, u32[]{:S(2)}) collective-permute-start(bf16[256,256]{1,0:T(8,128)(2,1)S(1)} %bitcast.14), channel_id=1, source_target_pairs={{32,0},{64,32},{96,64},{128,96},{160,128},{192,160},{224,192},{256... | collective-permute-start | bytes 393224 | tf_op jit(solution)/shard_map/ppermute | solution.py:362
  74.1 6.4 %copy-start.2 = (bf16[128,256]{1,0:T(8,128)(2,1)}, bf16[128,256]{1,0:T(8,128)(2,1)S(1)}, u32[]{:S(2)}) copy-start(bf16[128,256]{1,0:T(8,128)(2,1)S(1)} %collective-permute-done.4.z3_ref) | copy-start | bytes 196612
  80.5 0.6 copy-start.3
  81.1 0.6 copy-start.1
  96.6 0.6 copy-start.6
  96.6 0.7 copy-start.8
  120.8 27.3 %copy-start.7 = (bf16[256,256]{1,0:T(8,128)(2,1)S(1)}, bf16[256,256]{1,0:T(8,128)(2,1)}, u32[]{:S(2)}) copy-start(bf16[256,256]{1,0:T(8,128)(2,1)} %get-tuple-element.35) | copy-start | bytes 393220
  120.8 29.2 %copy-start.10 = (bf16[128,256]{1,0:T(8,128)(2,1)S(1)}, bf16[128,256]{1,0:T(8,128)(2,1)}, u32[]{:S(2)}) copy-start(bf16[128,256]{1,0:T(8,128)(2,1)} %get-tuple-element.36) | copy-start | bytes 196612
  120.8 33.5 %copy-start.9 = (bf16[128,256]{1,0:T(8,128)(2,1)S(1)}, bf16[128,256]{1,0:T(8,128)(2,1)}, u32[]{:S(2)}) copy-start(bf16[128,256]{1,0:T(8,128)(2,1)} %get-tuple-element.37) | copy-start | bytes 196612
  120.9 36.9 %copy-start.5 = (bf16[256,256]{1,0:T(8,128)(2,1)S(1)}, bf16[256,256]{1,0:T(8,128)(2,1)}, u32[]{:S(2)}) copy-start(bf16[256,256]{1,0:T(8,128)(2,1)} %get-tuple-element.33) | copy-start | bytes 393220
  120.9 43.7 %copy-start.4 = (bf16[256,256]{1,0:T(8,128)(2,1)S(1)}, bf16[256,256]{1,0:T(8,128)(2,1)}, u32[]{:S(2)}) copy-start(bf16[256,256]{1,0:T(8,128)(2,1)} %get-tuple-element.34) | copy-start | bytes 393220
  120.9 83.8 %all-to-all-start.2 = ((bf16[32,64,256]{2,1,0:T(8,128)(2,1)}), bf16[32,64,256]{2,1,0:T(8,128)(2,1)S(1)}, u32[]{:S(2)}, u32[]{:S(2)}) async-start(bf16[32,64,256]{2,1,0:T(8,128)(2,1)} %bitcast.12), calls=%async_computation.2 | async-start | bytes 2097152 | tf_op jit(solution)/shard_map/all_to_all | solution.py:358
  148.1 17.8 %collective-permute-start.7 = (bf16[256,256]{1,0:T(8,128)(2,1)S(1)}, bf16[256,256]{1,0:T(8,128)(2,1)S(1)}, u32[]{:S(2)}, u32[]{:S(2)}) collective-permute-start(bf16[256,256]{1,0:T(8,128)(2,1)S(1)} %copy-done.7), channel_id=1, source_target_pairs={{0,128},{128,0},{256,384},{384,256},{1,129},{129,1},{257,385},{385... | collective-permute-start | bytes 393224 | tf_op jit(solution)/shard_map/ppermute | solution.py:365
  150.1 15.8 %collective-permute-start.8 = (bf16[128,256]{1,0:T(8,128)(2,1)S(1)}, bf16[128,256]{1,0:T(8,128)(2,1)S(1)}, u32[]{:S(2)}, u32[]{:S(2)}) collective-permute-start(bf16[128,256]{1,0:T(8,128)(2,1)S(1)} %copy-done.10), channel_id=1, source_target_pairs={{0,256},{128,384},{256,0},{384,128},{1,257},{129,385},{257,1},{385... | collective-permute-start | bytes 196616 | tf_op jit(solution)/shard_map/ppermute | solution.py:365
  154.4 11.4 %collective-permute-start.9 = (bf16[128,256]{1,0:T(8,128)(2,1)S(1)}, bf16[128,256]{1,0:T(8,128)(2,1)S(1)}, u32[]{:S(2)}, u32[]{:S(2)}) collective-permute-start(bf16[128,256]{1,0:T(8,128)(2,1)S(1)} %copy-done.9), channel_id=1, source_target_pairs={{0,384},{128,256},{256,128},{384,0},{1,385},{129,257},{257,129},{3... | collective-permute-start | bytes 196616 | tf_op jit(solution)/shard_map/ppermute | solution.py:365
  157.7 26.8 %collective-permute-start.5 = (bf16[256,256]{1,0:T(8,128)(2,1)S(1)}, bf16[256,256]{1,0:T(8,128)(2,1)S(1)}, u32[]{:S(2)}, u32[]{:S(2)}) collective-permute-start(bf16[256,256]{1,0:T(8,128)(2,1)S(1)} %copy-done.5), channel_id=1, source_target_pairs={{0,32},{32,64},{64,96},{96,128},{128,160},{160,192},{192,224},{224... | collective-permute-start | bytes 393224 | tf_op jit(solution)/shard_map/ppermute | solution.py:362
  164.5 20.0 %collective-permute-start.6 = (bf16[256,256]{1,0:T(8,128)(2,1)S(1)}, bf16[256,256]{1,0:T(8,128)(2,1)S(1)}, u32[]{:S(2)}, u32[]{:S(2)}) collective-permute-start(bf16[256,256]{1,0:T(8,128)(2,1)S(1)} %copy-done.4), channel_id=1, source_target_pairs={{32,0},{64,32},{96,64},{128,96},{160,128},{192,160},{224,192},{256... | collective-permute-start | bytes 393224 | tf_op jit(solution)/shard_map/ppermute | solution.py:362
  167.7 34.1 %collective-permute-start.10 = (bf16[256,256]{1,0:T(8,128)(2,1)}, bf16[256,256]{1,0:T(8,128)(2,1)S(1)}, u32[]{:S(2)}, u32[]{:S(2)}) collective-permute-start(bf16[256,256]{1,0:T(8,128)(2,1)} %get-tuple-element.40), channel_id=1, source_target_pairs={{0,32},{32,0},{64,96},{96,64},{1,33},{33,1},{65,97},{97,65},{2,34}... | collective-permute-start | bytes 393224 | tf_op jit(solution)/shard_map/ppermute | solution.py:365
  175.6 14.3 %collective-permute-start.11 = (bf16[128,256]{1,0:T(8,128)(2,1)}, bf16[128,256]{1,0:T(8,128)(2,1)S(1)}, u32[]{:S(2)}, u32[]{:S(2)}) collective-permute-start(bf16[128,256]{1,0:T(8,128)(2,1)} %get-tuple-element.41), channel_id=1, source_target_pairs={{0,64},{32,96},{64,0},{96,32},{1,65},{33,97},{65,1},{97,33},{2,66}... | collective-permute-start | bytes 196616 | tf_op jit(solution)/shard_map/ppermute | solution.py:365
  179.9 21.9 %collective-permute-start.12 = (bf16[128,256]{1,0:T(8,128)(2,1)}, bf16[128,256]{1,0:T(8,128)(2,1)S(1)}, u32[]{:S(2)}, u32[]{:S(2)}) collective-permute-start(bf16[128,256]{1,0:T(8,128)(2,1)} %get-tuple-element.42), channel_id=1, source_target_pairs={{0,96},{32,64},{64,32},{96,0},{1,97},{33,65},{65,33},{97,1},{2,98}... | collective-permute-start | bytes 196616 | tf_op jit(solution)/shard_map/ppermute | solution.py:365
  204.7 33.7 %all-to-all-start.3 = ((bf16[32,64,256]{2,1,0:T(8,128)(2,1)}), bf16[32,64,256]{2,1,0:T(8,128)(2,1)S(1)}, u32[]{:S(2)}, u32[]{:S(2)}) async-start(bf16[32,64,256]{2,1,0:T(8,128)(2,1)} %bitcast.11), calls=%async_computation.3 | async-start | bytes 2097152 | tf_op jit(solution)/shard_map/all_to_all | solution.py:358
